TPU v7x, 128 devices: a whole 4x4x4 slice. The times are simulated.
128 devices in a mesh: slab: 16 (over y, x_lo, core), head: 8 (over z, x_hi).
Axes of the slice: x: 4 (x_hi: 2, x_lo: 2; x = x_hi * 2 + x_lo), y: 4, z: 4, core: 2. Of those that a mesh axis runs over, the one named last changes fastest.
Arguments:
- hidden_states: bfloat16 [6144, 6144], P(('slab', 'head')), may hold values from -36 to 36
- qkv_weight: bfloat16 [3, 6144, 3072], P(None, None, 'head'), may hold values from -0.078125 to 0.078125
- out_grad: bfloat16 [6144, 3072], P('slab', 'head'), may hold values from -6 to 6
- tile_frame: int32 [48], replicated, may hold values from 0 to 2, as said below
- frame_band: int32 [24], P('head'), may hold values from 0 to 2
Outputs:
- attn_out: bfloat16 [6144, 3072], P('slab', 'head')
- grad_hidden: bfloat16 [6144, 6144], P(('slab', 'head'))
Inputs may be any that keep to these rules, and one draw needn't show every extreme that they name: `tile_frame`: the tiles of one frame are consecutive; tile 0 lies in frame 0, each tile lies in the frame of the tile before it or in the next one, and the last tile lies in frame 2.
All inputs are finite; a program needn't handle non-finite values.
Results may differ from a plain program's by a relative error of at most 0.03.
The roundings to bfloat16 on the way count: a program that leaves them out, or rounds other values in their place, can miss the bound.
Values may be sent and summed in bfloat16 or wider, within the bound.
No kernel may reach another device: no remote copies, remote signals or barrier semaphores. Data moves between devices by JAX's collectives and lax.ppermute only.
A program may use at most 192 MiB of HBM per device.

v0:
```python
import functools
import math

import jax
import jax.numpy as jnp
from jax import lax
from jax.experimental import pallas as pl
from jax.experimental.pallas import tpu as pltpu
from jax.sharding import PartitionSpec as P

TILE = 128
BF = jnp.bfloat16
F32 = jnp.float32
NT_DIMS = (((1,), (1,)), ((), ()))
FAR = 1e30
FROM = ((0, 1, 2, 3), (2, 0, 3, 1), (1, 3, 0, 2), (3, 2, 1, 0))
STEPS = (0, -1, 1, 2)


def params(mebibytes):
    return pltpu.CompilerParams(vmem_limit_bytes=mebibytes * 1024 * 1024)


def after(x, *others):
    return lax.optimization_barrier((x, others))[0]


def cost(micros):
    return pl.CostEstimate(flops=int(micros * 1.15e9), bytes_accessed=0, transcendentals=0)


def dot(a, b):
    return jnp.dot(a, b, preferred_element_type=F32)


def dot_nt(a, b):
    return lax.dot_general(a, b, NT_DIMS, preferred_element_type=F32)


def project_kernel(count, height, first, last, place, *refs):
    blocks, w_ref = refs[:count], refs[count]
    acc_in = None if first else refs[count + 1]
    outs, (rows, acc) = refs[count + (1 if first else 2) : -2], refs[-2:]
    step = pl.program_id(0)

    @pl.when(step == 0)
    def _():
        if first:
            acc[...] = jnp.zeros_like(acc)
        else:
            acc[...] = acc_in[...]

    i = 0
    for block in blocks:
        for r in range(0, block.shape[0], height):
            rows[pl.ds(pl.multiple_of(place[i] * height, 16), height), :] = block[r : r + height, :]
            i += 1
    side = dot(rows[...], jnp.concatenate([w_ref[c] for c in range(3)], axis=1))
    width = w_ref.shape[2]
    for c in range(3):
        acc[c] += side[:, c * width : (c + 1) * width]

    @pl.when(step == pl.num_programs(0) - 1)
    def _():
        if last:
            q_ref, kv_ref = outs
            q_ref[...] = acc[0].astype(BF)
            kv_ref[:, :width] = acc[1].astype(BF)
            kv_ref[:, width:] = acc[2].astype(BF)
        else:
            outs[0][...] = acc[...]


def project(place, blocks, weight, start, acc=None, last=False, chunk=1024):
    columns, width = blocks[0].shape[1], weight.shape[2]
    total = sum(b.shape[0] for b in blocks)
    height = total // place.shape[0]
    skip = start // chunk
    whole = pl.BlockSpec((3, total, width), lambda k, place: (0, 0, 0))
    if last:
        out_shape = (
            jax.ShapeDtypeStruct((total, width), BF),
            jax.ShapeDtypeStruct((total, 2 * width), BF),
        )
        out_specs = (
            pl.BlockSpec((total, width), lambda k, place: (0, 0)),
            pl.BlockSpec((total, 2 * width), lambda k, place: (0, 0)),
        )
    else:
        out_shape, out_specs = jax.ShapeDtypeStruct((3, total, width), F32), whole
    return pl.pallas_call(
        functools.partial(project_kernel, len(blocks), height, acc is None, last),
        out_shape=out_shape,
        grid_spec=pltpu.PrefetchScalarGridSpec(
            num_scalar_prefetch=1,
            grid=(columns // chunk,),
            in_specs=[pl.BlockSpec((b.shape[0], chunk), lambda k, place: (0, k)) for b in blocks]
            + [pl.BlockSpec((3, chunk, width), lambda k, place: (0, k + skip, 0))]
            + ([] if acc is None else [whole]),
            out_specs=out_specs,
            scratch_shapes=[pltpu.VMEM((total, chunk), BF), pltpu.VMEM((3, total, width), F32)],
        ),
        compiler_params=params(18),
        cost_estimate=cost(6),
        name="project",
    )(place, *blocks, weight, *([] if acc is None else [acc]))


def forward_kernel(scale2, q0, q1, q2, q3, g0, g1, g2, g3, kv0, kv1, kv2, kv3, bias, ot, stat, qs, gt, kv, vt):
    size, width = q0.shape
    heads = width // TILE
    for b, (q, g, k) in enumerate(((q0, g0, kv0), (q1, g1, kv1), (q2, g2, kv2), (q3, g3, kv3))):
        qs[b] = q[...]
        kv[b * size : (b + 1) * size, :] = k[:, :width]
        for h in range(heads):
            at = slice(h * TILE, (h + 1) * TILE)
            gt[b, h] = g[:, at].T
            vt[h, :, b * size : (b + 1) * size] = k[:, width + h * TILE : width + (h + 1) * TILE].T
    tiles = kv.shape[0] // TILE

    def step(b, carry):
        for h in range(heads):
            at = slice(h * TILE, (h + 1) * TILE)
            s = dot_nt(kv[:, at], qs[b, :, at])
            away = bias[b, h]
            peak = jnp.full((1, size), -FAR, F32)
            for t in range(tiles):
                top = jnp.max(s[t * TILE : (t + 1) * TILE], axis=0, keepdims=True) * scale2
                peak = jnp.maximum(peak, top + away[t : t + 1])
            total = jnp.zeros((1, size), F32)
            parts = []
            for t in range(tiles):
                base = jnp.where(away[t : t + 1] < 0, FAR, peak)
                p = jnp.exp2(s[t * TILE : (t + 1) * TILE] * scale2 - base)
                total = total + jnp.sum(p, axis=0, keepdims=True)
                parts.append(p.astype(BF))
            o = dot(vt[h], jnp.concatenate(parts, axis=0))
            stat[b, 3 * h : 3 * h + 1, :] = peak
            stat[b, 3 * h + 1 : 3 * h + 2, :] = total
            stat[b, 3 * h + 2 : 3 * h + 3, :] = jnp.sum(o * gt[b, h].astype(F32), axis=0, keepdims=True)
            ot[b, h] = (o * jnp.where(total > 0, 1.0 / total, 0.0)).astype(BF)
        return carry

    lax.fori_loop(0, 4, step, 0)


def forward(scale2, queries, grads, pairs, bias):
    size, width = queries[0].shape
    heads = width // TILE
    return pl.pallas_call(
        functools.partial(forward_kernel, scale2),
        out_shape=(
            jax.ShapeDtypeStruct((4, heads, TILE, size), BF),
            jax.ShapeDtypeStruct((4, 3 * heads, size), F32),
        ),
        scratch_shapes=[
            pltpu.VMEM((4, size, width), BF),
            pltpu.VMEM((4, heads, TILE, size), BF),
            pltpu.VMEM((4 * size, width), BF),
            pltpu.VMEM((heads, TILE, 4 * size), BF),
        ],
        compiler_params=params(24),
        cost_estimate=cost(17), name="forward",
    )(*queries, *grads, *pairs, bias)


def totals_kernel(s0, s1, s2, s3, lse_ref, delta_ref):
    heads = lse_ref.shape[1]
    sources = (s0, s1, s2, s3)
    for p in range(4):
        for h in range(heads):
            rows = [
                [s[FROM[j][p], 3 * h + i : 3 * h + i + 1, :] for i in range(3)]
                for j, s in enumerate(sources)
            ]
            peak = functools.reduce(jnp.maximum, [r[0] for r in rows])
            shrink = [jnp.exp2(r[0] - peak) for r in rows]
            total = sum(r[1] * f for r, f in zip(rows, shrink))
            lse_ref[p, h : h + 1, :] = peak + jnp.log2(total)
            delta_ref[p, h : h + 1, :] = sum(r[2] * f for r, f in zip(rows, shrink)) / total


def totals(stats):
    _, rows, size = stats[0].shape
    shape = jax.ShapeDtypeStruct((4, rows // 3, size), F32)
    return pl.pallas_call(totals_kernel, out_shape=(shape, shape), compiler_params=params(6), cost_estimate=cost(2), name="totals")(*stats)


def merge_kernel(o0, o1, o2, o3, s0, s1, s2, s3, out):
    heads = o0.shape[0]
    for h in range(heads):
        rows = [
            [s[FROM[j][0], 3 * h + i : 3 * h + i + 1, :] for i in range(2)]
            for j, s in enumerate((s0, s1, s2, s3))
        ]
        peak = functools.reduce(jnp.maximum, [r[0] for r in rows])
        shares = [r[1] * jnp.exp2(r[0] - peak) for r in rows]
        whole = sum(shares)
        o = sum(x[h].astype(F32) * (share / whole) for x, share in zip((o0, o1, o2, o3), shares))
        out[:, h * TILE : (h + 1) * TILE] = o.T.astype(BF)


def merge(outs, stats):
    heads, _, size = outs[0].shape
    return pl.pallas_call(
        merge_kernel,
        out_shape=jax.ShapeDtypeStruct((size, heads * TILE), BF),
        compiler_params=params(6),
        cost_estimate=cost(2), name="merge",
    )(*outs, *stats)


def backward_kernel(scale2, factor, count, chained, last, places, *refs):
    q_refs, refs = refs[:count], refs[count:]
    g_refs, refs = refs[:count], refs[count:]
    (kv_a, kv_b, lse, delta, bias), refs = refs[:5], refs[5:]
    if chained:
        (dq_in, dk_in, dv_in), refs = refs[:3], refs[3:]
    else:
        dq_in = dk_in = dv_in = None
    outs, (qs, gs, ks, vs, kt, dk, dv) = refs[:-7], refs[-7:]
    finish = dq_in is not None
    dq_out = outs[0]
    size, width = q_refs[0].shape
    heads = width // TILE
    for b in range(count):
        qs[b] = q_refs[b][...]
        gs[b] = g_refs[b][...]
    for i, k in enumerate((kv_a, kv_b)):
        ks[i * size : (i + 1) * size, :] = k[:, :width]
        vs[i * size : (i + 1) * size, :] = k[:, width:]
        for h in range(heads):
            kt[h, :, i * size : (i + 1) * size] = k[:, h * TILE : (h + 1) * TILE].T
    if dk_in is None:
        dk[...] = jnp.zeros_like(dk)
        dv[...] = jnp.zeros_like(dv)
    else:
        dk[...] = dk_in[...]
        dv[...] = dv_in[...]
    tiles = 2 * size // TILE

    def step(i, carry):
        b, h = i // heads, lax.rem(i, heads)
        p0 = places + b
        at = pl.ds(pl.multiple_of(h * TILE, TILE), TILE)
        q, g = qs[b, :, at], gs[b, :, at]
        s = dot_nt(ks[:, at], q)
        dp = dot_nt(vs[:, at], g)
        away, top, shift = bias[p0, h], lse[p0, pl.ds(h, 1)], delta[p0, pl.ds(h, 1)]
        probs, grads = [], []
        for t in range(tiles):
            rows = slice(t * TILE, (t + 1) * TILE)
            base = jnp.where(away[t : t + 1] < 0, FAR, top)
            p = jnp.exp2(s[rows] * scale2 - base)
            probs.append(p.astype(BF))
            grads.append((p * (dp[rows] - shift)).astype(BF))
        p = jnp.concatenate(probs, axis=0)
        ds = jnp.concatenate(grads, axis=0)
        dv[:, at] += dot(p, g)
        dk[:, at] += dot(ds, q)
        dq = dot(kt[h], ds)
        if finish:
            dq_out[b, :, at] = ((dq_in[p0, h] + dq) * factor).T.astype(BF)
        else:
            dq_out[b, h] = dq
        return carry

    lax.fori_loop(0, count * heads, step, 0)
    if last:
        for i, out in enumerate(outs[1:]):
            rows = slice(i * size, (i + 1) * size)
            out[:, :width] = (dk[rows] * factor).astype(BF)
            out[:, width:] = dv[rows].astype(BF)
    else:
        outs[1][...] = dk[...]
        outs[2][...] = dv[...]


def backward(scale2, factor, queries, grads, pairs, lse, delta, bias, places=0, dq=None, sums=None, last=True):
    size, width = queries[0].shape
    heads, count = width // TILE, len(queries)
    if last:
        tail = (jax.ShapeDtypeStruct((size, 2 * width), BF),) * 2
    else:
        tail = (jax.ShapeDtypeStruct((2 * size, width), F32),) * 2
    if dq is None:
        head = jax.ShapeDtypeStruct((count, heads, TILE, size), F32)
    else:
        head = jax.ShapeDtypeStruct((count, size, width), BF)
    chained = dq is not None
    extra = [dq, *sums] if sums is not None else ([dq] if chained else [])

    def kernel(*refs):
        refs = list(refs)
        if chained and sums is None:
            at = 2 * count + 6
            refs[at:at] = [None, None]
        backward_kernel(scale2, factor, count, chained, last, places, *refs)

    return pl.pallas_call(
        kernel,
        out_shape=(head, *tail),
        scratch_shapes=[
            pltpu.VMEM((count, size, width), BF),
            pltpu.VMEM((count, size, width), BF),
            pltpu.VMEM((2 * size, width), BF),
            pltpu.VMEM((2 * size, width), BF),
            pltpu.VMEM((heads, TILE, 2 * size), BF),
            pltpu.VMEM((2 * size, width), F32),
            pltpu.VMEM((2 * size, width), F32),
        ],
        compiler_params=params(26),
        cost_estimate=cost(4 * count), name="backward",
    )(*queries, *grads, *pairs, lse, delta, bias, *extra)


def spread_kernel(height, place, dq, dkv, w_ref, *refs):
    outs, rows = refs[:-1], refs[-1]
    width = dq.shape[1]

    @pl.when(pl.program_id(0) == 0)
    def _():
        for i in range(place.shape[0]):
            at = pl.ds(pl.multiple_of(place[i] * height, 16), height)
            to = slice(i * height, (i + 1) * height)
            rows[to, :width] = dq[at, :]
            rows[to, width:] = dkv[at, :]

    total = sum(dot_nt(rows[:, c * width : (c + 1) * width], w_ref[c]) for c in range(3)).astype(BF)
    at = 0
    for out in outs:
        out[...] = total[at : at + out.shape[0]]
        at += out.shape[0]


def spread(place, dq, dkv, weight, start, columns, sizes, chunk=1024):
    total, width = dq.shape
    height = total // place.shape[0]
    skip = start // chunk
    return pl.pallas_call(
        functools.partial(spread_kernel, height),
        out_shape=tuple(jax.ShapeDtypeStruct((n * height, columns), BF) for n in sizes),
        grid_spec=pltpu.PrefetchScalarGridSpec(
            num_scalar_prefetch=1,
            grid=(columns // chunk,),
            in_specs=[
                pl.BlockSpec((total, width), lambda k, place: (0, 0)),
                pl.BlockSpec((total, 2 * width), lambda k, place: (0, 0)),
                pl.BlockSpec((3, chunk, width), lambda k, place: (0, k + skip, 0)),
            ],
            out_specs=tuple(pl.BlockSpec((n * height, chunk), lambda k, place: (0, k)) for n in sizes),
            scratch_shapes=[pltpu.VMEM((total, 3 * width), BF)],
        ),
        compiler_params=params(20),
        cost_estimate=cost(0.3),
        name="spread",
    )(place, dq, dkv, weight)


def body(hidden_states, qkv_weight, out_grad, tile_frame, frame_band):
    heads = frame_band.shape[0]
    width = qkv_weight.shape[2]
    head_dim = width // heads
    factor = 1.0 / math.sqrt(head_dim)
    scale2 = factor * math.log2(math.e)
    slabs, shards = lax.axis_size("slab"), lax.axis_size("head")
    slab, shard = lax.axis_index("slab"), lax.axis_index("head")
    height, model = hidden_states.shape
    part = model // 3
    slab_tiles = tile_frame.shape[0] // slabs

    def along_y(x, k):
        return lax.ppermute(x, "slab", [(i, (i + 4 * k) % slabs) for i in range(slabs)])

    def across_x(x):
        return lax.ppermute(x, "slab", [(i, i ^ 2) for i in range(slabs)])

    def across_core(x):
        return lax.ppermute(x, "slab", [(i, i ^ 1) for i in range(slabs)])

    def along_z(x, k):
        return lax.ppermute(x, "head", [(i, (i + 2 * k) % shards) for i in range(shards)])

    def across_far(x):
        return lax.ppermute(x, "head", [(i, i ^ 1) for i in range(shards)])

    z, far = shard // 2, shard % 2
    def places(shifts):
        return jnp.stack([((z + dz) % 4) * 2 + (far ^ dx) for dz, dx in shifts]).astype(jnp.int32)

    by_z = places([(dz, dx) for dz in STEPS for dx in (0, 1)])
    by_x = places([(dz, dx) for dx in (0, 1) for dz in STEPS])

    y, low = slab // 4, slab % 4
    frames = tile_frame.reshape(slabs, slab_tiles)
    query_frames = jnp.stack([frames[((y + d) % 4) * 4 + low] for d in STEPS])
    key_frames = jnp.concatenate([frames[y * 4 + (low ^ d)] for d in (0, 1, 2, 3)])
    distance = jnp.abs(query_frames[:, None, :] - key_frames[None, :, None])
    inside = distance[:, None] <= frame_band[None, :, None, None]
    bias = jnp.repeat(jnp.where(inside, 0.0, -FAR).astype(F32), TILE, axis=3)

    c, a, b = (hidden_states[:, i * part : (i + 1) * part] for i in range(3))
    up_c, down_c, two_c = along_z(c, 1), along_z(c, -1), along_z(c, 2)
    far_a = across_far(a)
    all_c = jnp.concatenate([c, up_c, down_c, two_c])
    far_c = across_far(all_c)
    pair_a = after(jnp.concatenate([a, far_a]), all_c)
    up_a, down_a = along_z(pair_a, 1), along_z(pair_a, -1)
    b = after(b, far_a, up_c)
    pair_b = jnp.concatenate([b, across_far(b)])
    down_b = along_z(pair_b, -1)
    up_b = along_z(after(pair_b, up_a), 1)
    two_a, two_b = along_z(up_a, 1), along_z(down_b, -1)
    grads = [out_grad, along_y(after(out_grad, up_c), 1)]
    grads.append(along_y(after(out_grad, grads[1]), -1))
    grads.append(along_y(after(out_grad, grads[2]), 2))

    streamed = pltpu.with_memory_space_constraint(qkv_weight, pltpu.HBM)
    acc = project(by_x, [all_c, far_c], streamed, 0)
    acc = project(by_z, [pair_a, up_a, down_a, two_a], qkv_weight, part, acc)
    acc, bias, grads[1:] = lax.optimization_barrier((acc, bias, grads[1:]))
    queries_own, pair_own = project(
        by_z, [pair_b, up_b, down_b, two_b], qkv_weight, 2 * part, acc, True
    )

    pair_x = across_x(pair_own)
    queries = [queries_own, along_y(queries_own, 1), along_y(queries_own, -1), along_y(queries_own, 2)]
    pair_x, queries[1:] = after((pair_x, queries[1:]), pair_own)
    pairs = [pair_own, across_core(pair_own), pair_x, across_core(pair_x)]

    out_t, stat = forward(scale2, queries, grads, pairs, bias)
    stats = [stat, along_y(stat, 1), along_y(stat, -1), along_y(stat, 2)]
    lse, delta = totals(stats)

    tiles = 2 * slab_tiles
    back = functools.partial(backward, scale2, factor)
    out_t = after(out_t, lse)
    outs = [out_t[0], along_y(out_t[2], 1), along_y(out_t[1], -1), along_y(out_t[3], 2)]
    dq, dx, dxc = back(queries, grads, pairs[2:], lse, delta, bias[:, :, tiles:])
    dq, dx, dxc, outs = lax.optimization_barrier((dq, dx, dxc, outs))
    dq, near = after((dq, dx + across_core(dxc)), dq)
    near = across_x(near)
    close = bias[:, :, :tiles]
    dqs, *sums = back(queries[1:], grads[1:], pairs[:2], lse, delta, close, 1, dq, None, False)
    got = [along_y(dqs[1], 1), along_y(dqs[0], -1), along_y(dqs[2], 2)]
    attn_out = merge(outs, stats)
    dq, near, attn_out = after((dq, near, attn_out), dqs)
    dq0, down_own, down_core = back(queries[:1], grads[:1], pairs[:2], lse, delta, close, 0, dq, sums)
    down_core, got = after((down_core, got), dq0)
    pair_grad = (
        down_own.astype(F32) + across_core(down_core).astype(F32) + near.astype(F32)
    ).astype(BF)
    query_grad = sum(x.astype(F32) for x in (dq0[0], *got)).astype(BF)

    send = functools.partial(spread, dkv=pair_grad, weight=qkv_weight, columns=part)
    own_a, prev_a, succ_a, out_a = send(by_z, query_grad, start=part, sizes=(2, 2, 2, 2))
    got_a, from_a = along_z(out_a, 1), along_z(prev_a, -1)
    own_c, prev_c, succ_c, out_c, other_c = send(
        by_x, after(query_grad, own_a), start=0, sizes=(1, 1, 1, 1, 4)
    )
    came_c = across_far(other_c)
    own_b, prev_b, succ_b, out_b = send(
        by_z, after(query_grad, own_c), start=2 * part, sizes=(2, 2, 2, 2)
    )
    got_b, from_b = along_z(out_b, -1), along_z(succ_b, 1)
    back_a = along_z(succ_a + got_a, 1)
    back_b = along_z(prev_b + got_b, -1)
    came_c = after(came_c, got_b)
    own_c, prev_c, succ_c, out_c = (
        (x.astype(F32) + came_c[i * height : (i + 1) * height].astype(F32)).astype(BF)
        for i, x in enumerate((own_c, prev_c, succ_c, out_c))
    )
    sums_c = (own_c, along_z(succ_c, 1), along_z(prev_c, -1), along_z(out_c, 2))
    done = [sum(x.astype(F32) for x in sums_c).astype(BF)]
    for own, one, other in ((own_a, from_a, back_a), (own_b, from_b, back_b)):
        total = own.astype(F32) + one.astype(F32) + other.astype(F32)
        rest = across_far(total[height:].astype(BF))
        done.append((total[:height] + rest.astype(F32)).astype(BF))
    return (attn_out, jnp.concatenate(done, axis=1))


def solution(mesh):
    placed = (P(("slab", "head"), None), P(None, None, "head"), P("slab", "head"), P(), P("head"))
    return jax.shard_map(
        body,
        mesh=mesh,
        in_specs=placed,
        out_specs=(P("slab", "head"), P(("slab", "head"), None)),
        check_vma=False,
    )
```

profile of v0, /device:TPU:0, one launch (start us, length us, event | category | flops | bytes accessed | tf_op | source)
XLA Modules:
  0.0 207.8 jit_solution(17974927339773677046)
XLA Ops:
  0.6 1.2 fusion.9
  1.8 4.0 %collective-permute-start.4 = (bf16[48,2048]{1,0:T(8,128)(2,1)S(1)}, bf16[48,2048]{1,0:T(8,128)(2,1)S(1)}, u32[]{:S(2)}, u32[]{:S(2)}) collective-permute-start(bf16[48,2048]{1,0:T(8,128)(2,1)S(1)} %get-tuple-element.138), channel_id=1, source_target_pairs={{0,4},{1,5},{2,6},{3,7},{4,0},{5,1},{6,2},{7,3},{8,12},{9,13},{10,... | collective-permute-start | bytes 589832 | tf_op jit(solution)/shard_map/ppermute | solution.py:382
  6.6 1.3 collective-permute-start.1
  7.9 3.0 %collective-permute-start = (bf16[48,2048]{1,0:T(8,128)(2,1)S(1)}, bf16[48,2048]{1,0:T(8,128)(2,1)S(1)}, u32[]{:S(2)}, u32[]{:S(2)}) collective-permute-start(bf16[48,2048]{1,0:T(8,128)(2,1)S(1)} %get-tuple-element.140), channel_id=1, source_target_pairs={{0,1},{1,0},{2,3},{3,2},{4,5},{5,4},{6,7},{7,6},{8,9},{9,8},{10,11... | collective-permute-start | bytes 589832 | tf_op jit(solution)/shard_map/ppermute | solution.py:385
  11.1 3.9 %collective-permute-done.1 = bf16[48,2048]{1,0:T(8,128)(2,1)S(1)} collective-permute-done((bf16[48,2048]{1,0:T(8,128)(2,1)S(1)}, bf16[48,2048]{1,0:T(8,128)(2,1)S(1)}, u32[]{:S(2)}, u32[]{:S(2)}) %collective-permute-start.1) | collective-permute-done | bytes 196640 | tf_op jit(solution)/shard_map/ppermute | solution.py:382
  15.2 3.0 %collective-permute-start.2 = (bf16[48,2048]{1,0:T(8,128)(2,1)S(1)}, bf16[48,2048]{1,0:T(8,128)(2,1)S(1)}, u32[]{:S(2)}, u32[]{:S(2)}) collective-permute-start(bf16[48,2048]{1,0:T(8,128)(2,1)S(1)} %get-tuple-element.65), channel_id=1, source_target_pairs={{0,1},{1,0},{2,3},{3,2},{4,5},{5,4},{6,7},{7,6},{8,9},{9,8},{10,11... | collective-permute-start | bytes 589832 | tf_op jit(solution)/shard_map/ppermute | solution.py:385
  18.2 1.6 collective-permute-start.12
  20.5 1.6 collective-permute-start.5
  22.1 1.4 collective-permute-done.2
  23.6 1.6 collective-permute-start.7
  25.1 2.3 %collective-permute-done.12.g1.refs_5_.refs_3_ = bf16[384,384]{1,0:T(8,128)(2,1)S(1)} collective-permute-done((bf16[384,384]{1,0:T(8,128)(2,1)}, bf16[384,384]{1,0:T(8,128)(2,1)S(1)}, u32[]{:S(2)}, u32[]{:S(2)}) %collective-permute-start.12) | collective-permute-done | bytes 294944 | tf_op jit(solution)/shard_map/ppermute | solution.py:373
  28.2 1.7 collective-permute-start.13
  30.3 0.9 broadcast_in_dim.17
  31.3 1.9 reshape.18
  33.2 2.0 collective-permute-start.9
  35.3 1.9 collective-permute-start.10
  37.2 1.3 collective-permute-start.8
  38.5 1.1 collective-permute-done.11.refs_1_
  39.6 3.2 %collective-permute-start.14 = (bf16[384,384]{1,0:T(8,128)(2,1)}, bf16[384,384]{1,0:T(8,128)(2,1)S(1)}, u32[]{:S(2)}, u32[]{:S(2)}) collective-permute-start(bf16[384,384]{1,0:T(8,128)(2,1)} %refs_1_.1), channel_id=1, source_target_pairs={{0,64},{8,72},{16,80},{24,88},{32,96},{40,104},{48,112},{56,120},{... | collective-permute-start | bytes 884744 | tf_op jit(solution)/shard_map/ppermute | solution.py:373
  42.8 5.1 %project.3.refs_5_ = f32[3,384,384]{2,1,0:T(8,128)S(1)} custom-call(s32[8]{0:T(128)S(1)} %stack.50.place, bf16[192,2048]{1,0:T(8,128)(2,1)S(1)} %pad_maximum_fusion.refs_0_, bf16[192,2048]{1,0:T(8,128)(2,1)} %collective-permute-done.11.refs_1_, bf16[3,6144,384]{2,1,0:T(8,128)(2,1)} %w_ref.5), custom_call_target="tpu_custom_call" | custom-call | flops 6899999744 | tf_op jit(solution)/shard_map/project/pallas_call | solution.py:91
  47.9 5.9 %collective-permute-done.10.refs_3_ = bf16[96,2048]{1,0:T(8,128)(2,1)S(1)} collective-permute-done((bf16[96,2048]{1,0:T(8,128)(2,1)}, bf16[96,2048]{1,0:T(8,128)(2,1)S(1)}, u32[]{:S(2)}, u32[]{:S(2)}) %collective-permute-start.10) | collective-permute-done | bytes 393248 | tf_op jit(solution)/shard_map/ppermute | solution.py:382
  53.8 4.2 %project.4.refs_5_ = f32[3,384,384]{2,1,0:T(8,128)S(1)} custom-call(s32[8]{0:T(128)S(1)} %stack.49.place, bf16[96,2048]{1,0:T(8,128)(2,1)S(1)} %pad_maximum_fusion.2.refs_0_, bf16[96,2048]{1,0:T(8,128)(2,1)} %collective-permute-done.5.refs_1_, bf16[96,2048]{1,0:T(8,128)(2,1)S(1)} %collective-permute-done.9.refs_2_, ...), custom_call_target="tpu_custom_call" | custom-call | flops 6899999744 | tf_op jit(solution)/shard_map/project/pallas_call | solution.py:91
  58.1 3.8 %project.5 = (bf16[384,384]{1,0:T(8,128)(2,1)S(1)}, bf16[384,768]{1,0:T(8,128)(2,1)S(1)}) custom-call(s32[8]{0:T(128)S(1)} %stack.49.place, bf16[96,2048]{1,0:T(8,128)(2,1)S(1)} %constant_dynamic-update-slice_fusion.refs_0_, bf16[96,2048]{1,0:T(8,128)(2,1)S(1)} %collective-permute-done.6.refs_1_, bf16[96,2048]{1,0:T(8,128)(2,1)S(1)} %collective-permute-done.7.refs_2_, ...), custom_call_target="tpu_custom_call" | custom-call | flops 6899999744 | tf_op jit(solution)/shard_map/project/pallas_call | solution.py:91
  62.0 1.0 collective-permute-start.15
  63.6 2.0 collective-permute-start.17
  65.6 7.2 %collective-permute-done.18.q3.refs_3_.refs_2_ = bf16[384,384]{1,0:T(8,128)(2,1)S(1)} collective-permute-done((bf16[384,384]{1,0:T(8,128)(2,1)S(1)}, bf16[384,384]{1,0:T(8,128)(2,1)S(1)}, u32[]{:S(2)}, u32[]{:S(2)}) %collective-permute-start.18) | collective-permute-done | bytes 294944 | tf_op jit(solution)/shard_map/ppermute | solution.py:373
  72.9 1.8 collective-permute-done.17.q2.refs_2_.refs_1_
  74.7 1.2 collective-permute-done.16.q1.refs_1_.refs_0_
  76.0 2.0 collective-permute-done.19.kv3.refs_9_
  77.9 14.8 %forward.1 = (bf16[4,3,128,384]{3,2,1,0:T(8,128)(2,1)S(1)}, f32[4,9,384]{2,1,0:T(8,128)S(1)}) custom-call(bf16[384,384]{1,0:T(8,128)(2,1)S(1)} %get-tuple-element.72.q0.refs_0_, bf16[384,384]{1,0:T(8,128)(2,1)S(1)} %collective-permute-done.16.q1.refs_1_.refs_0_, bf16[384,384]{1,0:T(8,128)(2,1)S(1)} %collective-permute-done.17.q2.refs_2_.refs_1_, ...), custom_call_target="tpu_custom_call" | custom-call | flops 19549999104 | tf_op jit(solution)/shard_map/forward/pallas_call | solution.py:150
  92.8 1.9 collective-permute-start.23
  94.6 1.4 collective-permute-start.22
  96.7 3.2 %collective-permute-done.23.s3 = f32[4,9,384]{2,1,0:T(8,128)S(1)} collective-permute-done((f32[4,9,384]{2,1,0:T(8,128)S(1)}, f32[4,9,384]{2,1,0:T(8,128)S(1)}, u32[]{:S(2)}, u32[]{:S(2)}) %collective-permute-start.23) | collective-permute-done | bytes 55328 | tf_op jit(solution)/shard_map/ppermute | solution.py:373
  100.1 1.8 collective-permute-done.21.s1
  102.1 1.3 collective-permute-start.26
  103.4 1.4 collective-permute-start.25
  105.4 12.8 %backward.3 = (f32[4,3,128,384]{3,2,1,0:T(8,128)S(1)}, bf16[384,768]{1,0:T(8,128)(2,1)S(1)}, bf16[384,768]{1,0:T(8,128)(2,1)S(1)}) custom-call(bf16[384,384]{1,0:T(8,128)(2,1)S(1)} %get-tuple-element.72.q0.refs_0_, bf16[384,384]{1,0:T(8,128)(2,1)S(1)} %collective-permute-done.16.q1.refs_1_.refs_0_, ...), custom_call_target="tpu_custom_call" | custom-call | flops 18400000000 | tf_op jit(solution)/shard_map/backward/pallas_call | solution.py:300
  118.3 1.1 merge.1
  119.4 0.9 collective-permute-done.27
  120.5 1.7 collective-permute-start.28
  122.2 10.6 %backward.4 = (bf16[3,384,384]{2,1,0:T(8,128)(2,1)S(1)}, f32[768,384]{1,0:T(8,128)S(1)}, f32[768,384]{1,0:T(8,128)S(1)}) custom-call(bf16[384,384]{1,0:T(8,128)(2,1)S(1)} %collective-permute-done.16.q1.refs_1_.refs_0_, bf16[384,384]{1,0:T(8,128)(2,1)S(1)} %collective-permute-done.17.q2.refs_2_.refs_1_, ...), custom_call_target="tpu_custom_call" | custom-call | flops 13799999488 | tf_op jit(solution)/shard_map/backward/pallas_call | solution.py:300
  132.9 2.4 %collective-permute-start.31 = (bf16[384,384]{1,0:T(8,128)(2,1)S(1)}, bf16[384,384]{1,0:T(8,128)(2,1)S(1)}, u32[]{:S(2)}, u32[]{:S(2)}) collective-permute-start(bf16[384,384]{1,0:T(8,128)(2,1)S(1)} %get-tuple-element.132), channel_id=1, source_target_pairs={{0,64},{8,72},{16,80},{24,88},{32,96},{40,104},{48,112},{56,120},{... | collective-permute-start | bytes 884744 | tf_op jit(solution)/shard_map/ppermute | solution.py:373
  135.3 0.9 collective-permute-start.30
  136.2 1.2 collective-permute-start.29
  137.3 4.6 %backward.5 = (bf16[1,384,384]{2,1,0:T(8,128)(2,1)S(1)}, bf16[384,768]{1,0:T(8,128)(2,1)S(1)}, bf16[384,768]{1,0:T(8,128)(2,1)S(1)}) custom-call(bf16[384,384]{1,0:T(8,128)(2,1)S(1)} %get-tuple-element.72.q0.refs_0_, bf16[384,384]{1,0:T(8,128)(2,1)} %refs_1_.1, bf16[384,768]{1,0:T(8,128)(2,1)S(1)} %get-tuple-element.73.kv0.refs_6_.refs_2_, ...), custom_call_target="tpu_custom_call" | custom-call | flops 4600000000 | tf_op jit(solution)/shard_map/backward/pallas_call | solution.py:300
  141.9 2.5 %collective-permute-done.31 = bf16[384,384]{1,0:T(8,128)(2,1)S(1)} collective-permute-done((bf16[384,384]{1,0:T(8,128)(2,1)S(1)}, bf16[384,384]{1,0:T(8,128)(2,1)S(1)}, u32[]{:S(2)}, u32[]{:S(2)}) %collective-permute-start.31) | collective-permute-done | bytes 294944 | tf_op jit(solution)/shard_map/ppermute | solution.py:373
  144.4 5.1 %collective-permute-done.30 = bf16[384,384]{1,0:T(8,128)(2,1)S(1)} collective-permute-done((bf16[384,384]{1,0:T(8,128)(2,1)S(1)}, bf16[384,384]{1,0:T(8,128)(2,1)S(1)}, u32[]{:S(2)}, u32[]{:S(2)}) %collective-permute-start.30) | collective-permute-done | bytes 294944 | tf_op jit(solution)/shard_map/ppermute | solution.py:373
  149.7 1.8 collective-permute-done.32
  151.8 4.1 %spread.3 = (bf16[96,2048]{1,0:T(8,128)(2,1)S(1)}, bf16[96,2048]{1,0:T(8,128)(2,1)S(1)}, bf16[96,2048]{1,0:T(8,128)(2,1)S(1)}, bf16[96,2048]{1,0:T(8,128)(2,1)S(1)}) custom-call(s32[8]{0:T(128)S(1)} %stack.49.place, bf16[384,384]{1,0:T(8,128)(2,1)S(1)} %fusion.2.dq, bf16[384,768]{1,0:T(8,128)(2,1)S(1)} %add_convert_fusion.dkv, bf16[3,6144,384]{2,1,0:T(8,128)(2,1)S(1)} %bitcast.36), custom_call_target="tpu_custom_call" | custom-call | flops 345000000 | tf_op jit(solution)/shard_map/spread/pallas_call | solution.py:340
  155.9 4.1 %spread.4 = (bf16[48,2048]{1,0:T(8,128)(2,1)S(1)}, bf16[48,2048]{1,0:T(8,128)(2,1)S(1)}, bf16[48,2048]{1,0:T(8,128)(2,1)S(1)}, bf16[48,2048]{1,0:T(8,128)(2,1)S(1)}, bf16[192,2048]{1,0:T(8,128)(2,1)S(1)}) custom-call(s32[8]{0:T(128)S(1)} %stack.50.place, bf16[384,384]{1,0:T(8,128)(2,1)S(1)} %fusion.2.dq, bf16[384,768]{1,0:T(8,128)(2,1)S(1)} %add_convert_fusion.dkv, ...), custom_call_target="tpu_custom_call" | custom-call | flops 345000000 | tf_op jit(solution)/shard_map/spread/pallas_call | solution.py:340
  159.9 1.5 collective-permute-start.33
  161.5 4.1 %spread.5 = (bf16[96,2048]{1,0:T(8,128)(2,1)S(1)}, bf16[96,2048]{1,0:T(8,128)(2,1)S(1)}, bf16[96,2048]{1,0:T(8,128)(2,1)S(1)}, bf16[96,2048]{1,0:T(8,128)(2,1)S(1)}) custom-call(s32[8]{0:T(128)S(1)} %stack.49.place, bf16[384,384]{1,0:T(8,128)(2,1)S(1)} %fusion.2.dq, bf16[384,768]{1,0:T(8,128)(2,1)S(1)} %add_convert_fusion.dkv, bf16[3,6144,384]{2,1,0:T(8,128)(2,1)S(1)} %bitcast.36), custom_call_target="tpu_custom_call" | custom-call | flops 345000000 | tf_op jit(solution)/shard_map/spread/pallas_call | solution.py:340
  165.6 3.3 %collective-permute-start.34 = (bf16[96,2048]{1,0:T(8,128)(2,1)S(1)}, bf16[96,2048]{1,0:T(8,128)(2,1)S(1)}, u32[]{:S(2)}, u32[]{:S(2)}) collective-permute-start(bf16[96,2048]{1,0:T(8,128)(2,1)S(1)} %get-tuple-element.117), channel_id=1, source_target_pairs={{0,6},{1,7},{2,0},{3,1},{4,2},{5,3},{6,4},{7,5},{8,14},{9,15},{10,... | collective-permute-start | bytes 1179656 | tf_op jit(solution)/shard_map/ppermute | solution.py:382
  168.9 1.9 collective-permute-start.42
  170.9 3.8 %collective-permute-done.39 = bf16[96,2048]{1,0:T(8,128)(2,1)S(1)} collective-permute-done((bf16[96,2048]{1,0:T(8,128)(2,1)S(1)}, bf16[96,2048]{1,0:T(8,128)(2,1)S(1)}, u32[]{:S(2)}, u32[]{:S(2)}) %collective-permute-start.39) | collective-permute-done | bytes 393248 | tf_op jit(solution)/shard_map/ppermute | solution.py:382
  174.9 3.5 %collective-permute-done.34 = bf16[96,2048]{1,0:T(8,128)(2,1)S(1)} collective-permute-done((bf16[96,2048]{1,0:T(8,128)(2,1)S(1)}, bf16[96,2048]{1,0:T(8,128)(2,1)S(1)}, u32[]{:S(2)}, u32[]{:S(2)}) %collective-permute-start.34) | collective-permute-done | bytes 393248 | tf_op jit(solution)/shard_map/ppermute | solution.py:382
  178.5 3.8 %collective-permute-start.43 = (bf16[96,2048]{1,0:T(8,128)(2,1)S(1)}, bf16[96,2048]{1,0:T(8,128)(2,1)S(1)}, u32[]{:S(2)}, u32[]{:S(2)}) collective-permute-start(bf16[96,2048]{1,0:T(8,128)(2,1)S(1)} %add.273), channel_id=1, source_target_pairs={{0,6},{1,7},{2,0},{3,1},{4,2},{5,3},{6,4},{7,5},{8,14},{9,15},{10,... | collective-permute-start | bytes 1179656 | tf_op jit(solution)/shard_map/ppermute | solution.py:382
  182.5 4.3 %collective-permute-done.38 = bf16[96,2048]{1,0:T(8,128)(2,1)S(1)} collective-permute-done((bf16[96,2048]{1,0:T(8,128)(2,1)S(1)}, bf16[96,2048]{1,0:T(8,128)(2,1)S(1)}, u32[]{:S(2)}, u32[]{:S(2)}) %collective-permute-start.38) | collective-permute-done | bytes 393248 | tf_op jit(solution)/shard_map/ppermute | solution.py:382
  186.8 1.9 collective-permute-start.37
  188.7 2.8 %collective-permute-done.40 = bf16[96,2048]{1,0:T(8,128)(2,1)S(1)} collective-permute-done((bf16[96,2048]{1,0:T(8,128)(2,1)S(1)}, bf16[96,2048]{1,0:T(8,128)(2,1)S(1)}, u32[]{:S(2)}, u32[]{:S(2)}) %collective-permute-start.40) | collective-permute-done | bytes 393248 | tf_op jit(solution)/shard_map/ppermute | solution.py:382
  191.7 2.6 %collective-permute-start.41 = (bf16[48,2048]{1,0:T(8,128)(2,1)S(1)}, bf16[48,2048]{1,0:T(8,128)(2,1)S(1)}, u32[]{:S(2)}, u32[]{:S(2)}) collective-permute-start(bf16[48,2048]{1,0:T(8,128)(2,1)S(1)} %slice.108), channel_id=1, source_target_pairs={{0,1},{1,0},{2,3},{3,2},{4,5},{5,4},{6,7},{7,6},{8,9},{9,8},{10,11... | collective-permute-start | bytes 589832 | tf_op jit(solution)/shard_map/ppermute | solution.py:385
  194.3 5.2 %collective-permute-done.43 = bf16[96,2048]{1,0:T(8,128)(2,1)S(1)} collective-permute-done((bf16[96,2048]{1,0:T(8,128)(2,1)S(1)}, bf16[96,2048]{1,0:T(8,128)(2,1)S(1)}, u32[]{:S(2)}, u32[]{:S(2)}) %collective-permute-start.43) | collective-permute-done | bytes 393248 | tf_op jit(solution)/shard_map/ppermute | solution.py:382
  199.7 2.2 %collective-permute-start.44 = (bf16[48,2048]{1,0:T(8,128)(2,1)S(1)}, bf16[48,2048]{1,0:T(8,128)(2,1)S(1)}, u32[]{:S(2)}, u32[]{:S(2)}) collective-permute-start(bf16[48,2048]{1,0:T(8,128)(2,1)S(1)} %slice.107), channel_id=1, source_target_pairs={{0,1},{1,0},{2,3},{3,2},{4,5},{5,4},{6,7},{7,6},{8,9},{9,8},{10,11... | collective-permute-start | bytes 589832 | tf_op jit(solution)/shard_map/ppermute | solution.py:385
  202.5 4.5 %collective-permute-done.44 = bf16[48,2048]{1,0:T(8,128)(2,1)S(1)} collective-permute-done((bf16[48,2048]{1,0:T(8,128)(2,1)S(1)}, bf16[48,2048]{1,0:T(8,128)(2,1)S(1)}, u32[]{:S(2)}, u32[]{:S(2)}) %collective-permute-start.44) | collective-permute-done | bytes 196640 | tf_op jit(solution)/shard_map/ppermute | solution.py:385
  (90 shorter events, 8.5 us)
Async XLA Ops:
  0.6 10.3 %copy-start.4 = (s32[48]{0:T(128)S(1)}, s32[48]{0:T(128)}, u32[]{:S(2)}) copy-start(s32[48]{0:T(128)} %param.8) | copy-start | bytes 580
  1.8 18.0 %collective-permute-start.4 = (bf16[48,2048]{1,0:T(8,128)(2,1)S(1)}, bf16[48,2048]{1,0:T(8,128)(2,1)S(1)}, u32[]{:S(2)}, u32[]{:S(2)}) collective-permute-start(bf16[48,2048]{1,0:T(8,128)(2,1)S(1)} %get-tuple-element.138), channel_id=1, source_target_pairs={{0,4},{1,5},{2,6},{3,7},{4,0},{5,1},{6,2},{7,3},{8,12},{9,13},{10,... | collective-permute-start | bytes 589832 | tf_op jit(solution)/shard_map/ppermute | solution.py:382
  5.8 13.9 %collective-permute-start.3 = (bf16[48,2048]{1,0:T(8,128)(2,1)S(1)}, bf16[48,2048]{1,0:T(8,128)(2,1)S(1)}, u32[]{:S(2)}, u32[]{:S(2)}) collective-permute-start(bf16[48,2048]{1,0:T(8,128)(2,1)S(1)} %get-tuple-element.138), channel_id=1, source_target_pairs={{0,6},{1,7},{2,0},{3,1},{4,2},{5,3},{6,4},{7,5},{8,14},{9,15},{10,... | collective-permute-start | bytes 589832 | tf_op jit(solution)/shard_map/ppermute | solution.py:382
  6.6 8.4 %collective-permute-start.1 = (bf16[48,2048]{1,0:T(8,128)(2,1)S(1)}, bf16[48,2048]{1,0:T(8,128)(2,1)S(1)}, u32[]{:S(2)}, u32[]{:S(2)}) collective-permute-start(bf16[48,2048]{1,0:T(8,128)(2,1)S(1)} %get-tuple-element.138), channel_id=1, source_target_pairs={{0,2},{1,3},{2,4},{3,5},{4,6},{5,7},{6,0},{7,1},{8,10},{9,11},{10,... | collective-permute-start | bytes 589832 | tf_op jit(solution)/shard_map/ppermute | solution.py:382
  7.9 7.3 %collective-permute-start = (bf16[48,2048]{1,0:T(8,128)(2,1)S(1)}, bf16[48,2048]{1,0:T(8,128)(2,1)S(1)}, u32[]{:S(2)}, u32[]{:S(2)}) collective-permute-start(bf16[48,2048]{1,0:T(8,128)(2,1)S(1)} %get-tuple-element.140), channel_id=1, source_target_pairs={{0,1},{1,0},{2,3},{3,2},{4,5},{5,4},{6,7},{7,6},{8,9},{9,8},{10,11... | collective-permute-start | bytes 589832 | tf_op jit(solution)/shard_map/ppermute | solution.py:385
  15.2 8.4 %collective-permute-start.2 = (bf16[48,2048]{1,0:T(8,128)(2,1)S(1)}, bf16[48,2048]{1,0:T(8,128)(2,1)S(1)}, u32[]{:S(2)}, u32[]{:S(2)}) collective-permute-start(bf16[48,2048]{1,0:T(8,128)(2,1)S(1)} %get-tuple-element.65), channel_id=1, source_target_pairs={{0,1},{1,0},{2,3},{3,2},{4,5},{5,4},{6,7},{7,6},{8,9},{9,8},{10,11... | collective-permute-start | bytes 589832 | tf_op jit(solution)/shard_map/ppermute | solution.py:385
  18.2 9.2 %collective-permute-start.12 = (bf16[384,384]{1,0:T(8,128)(2,1)}, bf16[384,384]{1,0:T(8,128)(2,1)S(1)}, u32[]{:S(2)}, u32[]{:S(2)}) collective-permute-start(bf16[384,384]{1,0:T(8,128)(2,1)} %refs_1_.1), channel_id=1, source_target_pairs={{0,32},{8,40},{16,48},{24,56},{32,64},{40,72},{48,80},{56,88},{64,... | collective-permute-start | bytes 884744 | tf_op jit(solution)/shard_map/ppermute | solution.py:373
  19.9 10.4 %copy-start.3 = (s32[3]{0:T(128)S(1)}, s32[3]{0:T(128)}, u32[]{:S(2)}) copy-start(s32[3]{0:T(128)} %param.9) | copy-start | bytes 40
  19.9 19.7 %collective-permute-start.11 = (bf16[192,2048]{1,0:T(8,128)(2,1)S(1)}, bf16[192,2048]{1,0:T(8,128)(2,1)}, u32[]{:S(2)}, u32[]{:S(2)}) collective-permute-start(bf16[192,2048]{1,0:T(8,128)(2,1)S(1)} %pad_maximum_fusion.refs_0_), channel_id=1, source_target_pairs={{0,1},{1,0},{2,3},{3,2},{4,5},{5,4},{6,7},{7,6},{8,9},{9,8},{10,11... | collective-permute-start | bytes 2359304 | tf_op jit(solution)/shard_map/ppermute | solution.py:385
  20.5 14.7 %collective-permute-start.5 = (bf16[96,2048]{1,0:T(8,128)(2,1)S(1)}, bf16[96,2048]{1,0:T(8,128)(2,1)}, u32[]{:S(2)}, u32[]{:S(2)}) collective-permute-start(bf16[96,2048]{1,0:T(8,128)(2,1)S(1)} %pad_maximum_fusion.2.refs_0_), channel_id=1, source_target_pairs={{0,2},{1,3},{2,4},{3,5},{4,6},{5,7},{6,0},{7,1},{8,10},{9,11},{10,... | collective-permute-start | bytes 1179656 | tf_op jit(solution)/shard_map/ppermute | solution.py:382
  23.6 11.7 %collective-permute-start.7 = (bf16[96,2048]{1,0:T(8,128)(2,1)S(1)}, bf16[96,2048]{1,0:T(8,128)(2,1)S(1)}, u32[]{:S(2)}, u32[]{:S(2)}) collective-permute-start(bf16[96,2048]{1,0:T(8,128)(2,1)S(1)} %constant_dynamic-update-slice_fusion.refs_0_), channel_id=1, source_target_pairs={{0,6},{1,7},{2,0},{3,1},{4,2},{5,3},{6,4},{7,5},{8,14},{9,15},{10,... | collective-permute-start | bytes 1179656 | tf_op jit(solution)/shard_map/ppermute | solution.py:382
  27.4 0.7 copy-start
  28.2 9.0 %collective-permute-start.13 = (bf16[384,384]{1,0:T(8,128)(2,1)}, bf16[384,384]{1,0:T(8,128)(2,1)}, u32[]{:S(2)}, u32[]{:S(2)}) collective-permute-start(bf16[384,384]{1,0:T(8,128)(2,1)} %refs_1_.1), channel_id=1, source_target_pairs={{0,96},{8,104},{16,112},{24,120},{32,0},{40,8},{48,16},{56,24},{64... | collective-permute-start | bytes 884744 | tf_op jit(solution)/shard_map/ppermute | solution.py:373
  31.3 22.5 %slice-start = ((s8[14155776]{0:T(1024)(128)(4,1)}), s8[1572864]{0:T(1024)(128)(4,1)S(1)}, s32[]{:S(2)}) async-start(s8[14155776]{0:T(1024)(128)(4,1)} %bitcast.35), calls=%async_computation | async-start | bytes 3145728
  33.2 20.6 %slice-start.1 = ((s8[14155776]{0:T(1024)(128)(4,1)}), s8[4194304]{0:T(1024)(128)(4,1)S(1)}, s32[]{:S(2)}) async-start(s8[14155776]{0:T(1024)(128)(4,1)} %bitcast.35), calls=%async_computation.1 | async-start | bytes 8388608
  33.2 20.6 %slice-start.2 = ((s8[14155776]{0:T(1024)(128)(4,1)}), s8[4194304]{0:T(1024)(128)(4,1)S(1)}, s32[]{:S(2)}) async-start(s8[14155776]{0:T(1024)(128)(4,1)} %bitcast.35), calls=%async_computation.2 | async-start | bytes 8388608
  33.2 20.6 %slice-start.3 = ((s8[14155776]{0:T(1024)(128)(4,1)}), s8[4194304]{0:T(1024)(128)(4,1)S(1)}, s32[]{:S(2)}) async-start(s8[14155776]{0:T(1024)(128)(4,1)} %bitcast.35), calls=%async_computation.3 | async-start | bytes 8388608
  33.2 14.6 %collective-permute-start.9 = (bf16[96,2048]{1,0:T(8,128)(2,1)S(1)}, bf16[96,2048]{1,0:T(8,128)(2,1)S(1)}, u32[]{:S(2)}, u32[]{:S(2)}) collective-permute-start(bf16[96,2048]{1,0:T(8,128)(2,1)S(1)} %pad_maximum_fusion.2.refs_0_), channel_id=1, source_target_pairs={{0,6},{1,7},{2,0},{3,1},{4,2},{5,3},{6,4},{7,5},{8,14},{9,15},{10,... | collective-permute-start | bytes 1179656 | tf_op jit(solution)/shard_map/ppermute | solution.py:382
  35.2 22.9 %collective-permute-start.6 = (bf16[96,2048]{1,0:T(8,128)(2,1)S(1)}, bf16[96,2048]{1,0:T(8,128)(2,1)S(1)}, u32[]{:S(2)}, u32[]{:S(2)}) collective-permute-start(bf16[96,2048]{1,0:T(8,128)(2,1)S(1)} %constant_dynamic-update-slice_fusion.refs_0_), channel_id=1, source_target_pairs={{0,2},{1,3},{2,4},{3,5},{4,6},{5,7},{6,0},{7,1},{8,10},{9,11},{10,... | collective-permute-start | bytes 1179656 | tf_op jit(solution)/shard_map/ppermute | solution.py:382
  35.3 18.6 %collective-permute-start.10 = (bf16[96,2048]{1,0:T(8,128)(2,1)}, bf16[96,2048]{1,0:T(8,128)(2,1)S(1)}, u32[]{:S(2)}, u32[]{:S(2)}) collective-permute-start(bf16[96,2048]{1,0:T(8,128)(2,1)} %collective-permute-done.5.refs_1_), channel_id=1, source_target_pairs={{0,2},{1,3},{2,4},{3,5},{4,6},{5,7},{6,0},{7,1},{8,10},{9,11},{10,... | collective-permute-start | bytes 1179656 | tf_op jit(solution)/shard_map/ppermute | solution.py:382
  37.2 20.9 %collective-permute-start.8 = (bf16[96,2048]{1,0:T(8,128)(2,1)S(1)}, bf16[96,2048]{1,0:T(8,128)(2,1)S(1)}, u32[]{:S(2)}, u32[]{:S(2)}) collective-permute-start(bf16[96,2048]{1,0:T(8,128)(2,1)S(1)} %collective-permute-done.7.refs_2_), channel_id=1, source_target_pairs={{0,6},{1,7},{2,0},{3,1},{4,2},{5,3},{6,4},{7,5},{8,14},{9,15},{10,... | collective-permute-start | bytes 1179656 | tf_op jit(solution)/shard_map/ppermute | solution.py:382
  39.6 18.5 %collective-permute-start.14 = (bf16[384,384]{1,0:T(8,128)(2,1)}, bf16[384,384]{1,0:T(8,128)(2,1)S(1)}, u32[]{:S(2)}, u32[]{:S(2)}) collective-permute-start(bf16[384,384]{1,0:T(8,128)(2,1)} %refs_1_.1), channel_id=1, source_target_pairs={{0,64},{8,72},{16,80},{24,88},{32,96},{40,104},{48,112},{56,120},{... | collective-permute-start | bytes 884744 | tf_op jit(solution)/shard_map/ppermute | solution.py:373
  58.0 17.9 %copy-start.2 = (f32[4,3,12,384]{3,0,2,1:T(4,128)S(1)}, f32[4,3,12,384]{3,0,2,1:T(4,128)}, u32[]{:S(2)}) copy-start(f32[4,3,12,384]{3,0,2,1:T(4,128)} %reshape.18) | copy-start | bytes 663556
  58.1 19.9 %copy-start.1 = (bf16[384,384]{1,0:T(8,128)(2,1)S(1)}, bf16[384,384]{1,0:T(8,128)(2,1)}, u32[]{:S(2)}) copy-start(bf16[384,384]{1,0:T(8,128)(2,1)} %copy-done) | copy-start | bytes 884740
  62.0 14.0 %collective-permute-start.15 = (bf16[384,768]{1,0:T(8,128)(2,1)S(1)}, bf16[384,768]{1,0:T(8,128)(2,1)S(1)}, u32[]{:S(2)}, u32[]{:S(2)}) collective-permute-start(bf16[384,768]{1,0:T(8,128)(2,1)S(1)} %get-tuple-element.73.kv0.refs_6_.refs_2_), channel_id=1, source_target_pairs={{0,16},{8,24},{16,0},{24,8},{32,48},{40,56},{48,32},{56,40},{64,80... | collective-permute-start | bytes 1769480 | tf_op jit(solution)/shard_map/ppermute | solution.py:376
  63.0 9.9 %collective-permute-start.18 = (bf16[384,384]{1,0:T(8,128)(2,1)S(1)}, bf16[384,384]{1,0:T(8,128)(2,1)S(1)}, u32[]{:S(2)}, u32[]{:S(2)}) collective-permute-start(bf16[384,384]{1,0:T(8,128)(2,1)S(1)} %get-tuple-element.72.q0.refs_0_), channel_id=1, source_target_pairs={{0,64},{8,72},{16,80},{24,88},{32,96},{40,104},{48,112},{56,120},{... | collective-permute-start | bytes 884744 | tf_op jit(solution)/shard_map/ppermute | solution.py:373
  63.6 11.1 %collective-permute-start.17 = (bf16[384,384]{1,0:T(8,128)(2,1)S(1)}, bf16[384,384]{1,0:T(8,128)(2,1)S(1)}, u32[]{:S(2)}, u32[]{:S(2)}) collective-permute-start(bf16[384,384]{1,0:T(8,128)(2,1)S(1)} %get-tuple-element.72.q0.refs_0_), channel_id=1, source_target_pairs={{0,96},{8,104},{16,112},{24,120},{32,0},{40,8},{48,16},{56,24},{64... | collective-permute-start | bytes 884744 | tf_op jit(solution)/shard_map/ppermute | solution.py:373
  65.5 10.4 %collective-permute-start.16 = (bf16[384,384]{1,0:T(8,128)(2,1)S(1)}, bf16[384,384]{1,0:T(8,128)(2,1)S(1)}, u32[]{:S(2)}, u32[]{:S(2)}) collective-permute-start(bf16[384,384]{1,0:T(8,128)(2,1)S(1)} %get-tuple-element.72.q0.refs_0_), channel_id=1, source_target_pairs={{0,32},{8,40},{16,48},{24,56},{32,64},{40,72},{48,80},{56,88},{64,... | collective-permute-start | bytes 884744 | tf_op jit(solution)/shard_map/ppermute | solution.py:373
  65.6 10.4 %collective-permute-start.20 = (bf16[384,768]{1,0:T(8,128)(2,1)S(1)}, bf16[384,768]{1,0:T(8,128)(2,1)S(1)}, u32[]{:S(2)}, u32[]{:S(2)}) collective-permute-start(bf16[384,768]{1,0:T(8,128)(2,1)S(1)} %get-tuple-element.73.kv0.refs_6_.refs_2_), channel_id=1, source_target_pairs={{0,8},{8,0},{16,24},{24,16},{32,40},{40,32},{48,56},{56,48},{64,72... | collective-permute-start | bytes 1769480 | tf_op jit(solution)/shard_map/ppermute | solution.py:379
  75.9 2.0 collective-permute-start.19
  92.8 7.1 %collective-permute-start.23 = (f32[4,9,384]{2,1,0:T(8,128)S(1)}, f32[4,9,384]{2,1,0:T(8,128)S(1)}, u32[]{:S(2)}, u32[]{:S(2)}) collective-permute-start(f32[4,9,384]{2,1,0:T(8,128)S(1)} %get-tuple-element.82.s0), channel_id=1, source_target_pairs={{0,64},{8,72},{16,80},{24,88},{32,96},{40,104},{48,112},{56,120},{... | collective-permute-start | bytes 165896 | tf_op jit(solution)/shard_map/ppermute | solution.py:373
  94.6 5.4 %collective-permute-start.22 = (f32[4,9,384]{2,1,0:T(8,128)S(1)}, f32[4,9,384]{2,1,0:T(8,128)S(1)}, u32[]{:S(2)}, u32[]{:S(2)}) collective-permute-start(f32[4,9,384]{2,1,0:T(8,128)S(1)} %get-tuple-element.82.s0), channel_id=1, source_target_pairs={{0,96},{8,104},{16,112},{24,120},{32,0},{40,8},{48,16},{56,24},{64... | collective-permute-start | bytes 165896 | tf_op jit(solution)/shard_map/ppermute | solution.py:373
  96.0 5.8 %collective-permute-start.21 = (f32[4,9,384]{2,1,0:T(8,128)S(1)}, f32[4,9,384]{2,1,0:T(8,128)S(1)}, u32[]{:S(2)}, u32[]{:S(2)}) collective-permute-start(f32[4,9,384]{2,1,0:T(8,128)S(1)} %get-tuple-element.82.s0), channel_id=1, source_target_pairs={{0,32},{8,40},{16,48},{24,56},{32,64},{40,72},{48,80},{56,88},{64,... | collective-permute-start | bytes 165896 | tf_op jit(solution)/shard_map/ppermute | solution.py:373
  102.1 16.1 %collective-permute-start.26 = (bf16[3,128,384]{2,1,0:T(8,128)(2,1)S(1)}, bf16[3,128,384]{2,1,0:T(8,128)(2,1)S(1)}, u32[]{:S(2)}, u32[]{:S(2)}) collective-permute-start(bf16[3,128,384]{2,1,0:T(8,128)(2,1)S(1)} %get-tuple-element.128), channel_id=1, source_target_pairs={{0,64},{8,72},{16,80},{24,88},{32,96},{40,104},{48,112},{56,120},{... | collective-permute-start | bytes 884744 | tf_op jit(solution)/shard_map/ppermute | solution.py:373
  103.4 14.9 %collective-permute-start.25 = (bf16[3,128,384]{2,1,0:T(8,128)(2,1)S(1)}, bf16[3,128,384]{2,1,0:T(8,128)(2,1)S(1)}, u32[]{:S(2)}, u32[]{:S(2)}) collective-permute-start(bf16[3,128,384]{2,1,0:T(8,128)(2,1)S(1)} %get-tuple-element.129), channel_id=1, source_target_pairs={{0,96},{8,104},{16,112},{24,120},{32,0},{40,8},{48,16},{56,24},{64... | collective-permute-start | bytes 884744 | tf_op jit(solution)/shard_map/ppermute | solution.py:373
  104.8 13.4 %collective-permute-start.24 = (bf16[3,128,384]{2,1,0:T(8,128)(2,1)S(1)}, bf16[3,128,384]{2,1,0:T(8,128)(2,1)S(1)}, u32[]{:S(2)}, u32[]{:S(2)}) collective-permute-start(bf16[3,128,384]{2,1,0:T(8,128)(2,1)S(1)} %get-tuple-element.130), channel_id=1, source_target_pairs={{0,32},{8,40},{16,48},{24,56},{32,64},{40,72},{48,80},{56,88},{64,... | collective-permute-start | bytes 884744 | tf_op jit(solution)/shard_map/ppermute | solution.py:373
  118.2 2.1 %collective-permute-start.27 = (bf16[384,768]{1,0:T(8,128)(2,1)S(1)}, bf16[384,768]{1,0:T(8,128)(2,1)S(1)}, u32[]{:S(2)}, u32[]{:S(2)}) collective-permute-start(bf16[384,768]{1,0:T(8,128)(2,1)S(1)} %get-tuple-element.92), channel_id=1, source_target_pairs={{0,8},{8,0},{16,24},{24,16},{32,40},{40,32},{48,56},{56,48},{64,72... | collective-permute-start | bytes 1769480 | tf_op jit(solution)/shard_map/ppermute | solution.py:379
  120.5 16.9 %collective-permute-start.28 = (bf16[384,768]{1,0:T(8,128)(2,1)S(1)}, bf16[384,768]{1,0:T(8,128)(2,1)S(1)}, u32[]{:S(2)}, u32[]{:S(2)}) collective-permute-start(bf16[384,768]{1,0:T(8,128)(2,1)S(1)} %add.255), channel_id=1, source_target_pairs={{0,16},{8,24},{16,0},{24,8},{32,48},{40,56},{48,32},{56,40},{64,80... | collective-permute-start | bytes 1769480 | tf_op jit(solution)/shard_map/ppermute | solution.py:376
  132.9 11.5 %collective-permute-start.31 = (bf16[384,384]{1,0:T(8,128)(2,1)S(1)}, bf16[384,384]{1,0:T(8,128)(2,1)S(1)}, u32[]{:S(2)}, u32[]{:S(2)}) collective-permute-start(bf16[384,384]{1,0:T(8,128)(2,1)S(1)} %get-tuple-element.132), channel_id=1, source_target_pairs={{0,64},{8,72},{16,80},{24,88},{32,96},{40,104},{48,112},{56,120},{... | collective-permute-start | bytes 884744 | tf_op jit(solution)/shard_map/ppermute | solution.py:373
  135.3 14.3 %collective-permute-start.30 = (bf16[384,384]{1,0:T(8,128)(2,1)S(1)}, bf16[384,384]{1,0:T(8,128)(2,1)S(1)}, u32[]{:S(2)}, u32[]{:S(2)}) collective-permute-start(bf16[384,384]{1,0:T(8,128)(2,1)S(1)} %get-tuple-element.133), channel_id=1, source_target_pairs={{0,96},{8,104},{16,112},{24,120},{32,0},{40,8},{48,16},{56,24},{64... | collective-permute-start | bytes 884744 | tf_op jit(solution)/shard_map/ppermute | solution.py:373
  136.2 13.4 %collective-permute-start.29 = (bf16[384,384]{1,0:T(8,128)(2,1)S(1)}, bf16[384,384]{1,0:T(8,128)(2,1)S(1)}, u32[]{:S(2)}, u32[]{:S(2)}) collective-permute-start(bf16[384,384]{1,0:T(8,128)(2,1)S(1)} %get-tuple-element.134), channel_id=1, source_target_pairs={{0,32},{8,40},{16,48},{24,56},{32,64},{40,72},{48,80},{56,88},{64,... | collective-permute-start | bytes 884744 | tf_op jit(solution)/shard_map/ppermute | solution.py:373
  149.6 2.0 collective-permute-start.32
  159.9 22.3 %collective-permute-start.33 = (bf16[192,2048]{1,0:T(8,128)(2,1)S(1)}, bf16[192,2048]{1,0:T(8,128)(2,1)S(1)}, u32[]{:S(2)}, u32[]{:S(2)}) collective-permute-start(bf16[192,2048]{1,0:T(8,128)(2,1)S(1)} %get-tuple-element.115), channel_id=1, source_target_pairs={{0,1},{1,0},{2,3},{3,2},{4,5},{5,4},{6,7},{7,6},{8,9},{9,8},{10,11... | collective-permute-start | bytes 2359304 | tf_op jit(solution)/shard_map/ppermute | solution.py:385
  161.5 13.2 %collective-permute-start.39 = (bf16[96,2048]{1,0:T(8,128)(2,1)S(1)}, bf16[96,2048]{1,0:T(8,128)(2,1)S(1)}, u32[]{:S(2)}, u32[]{:S(2)}) collective-permute-start(bf16[96,2048]{1,0:T(8,128)(2,1)S(1)} %get-tuple-element.124), channel_id=1, source_target_pairs={{0,2},{1,3},{2,4},{3,5},{4,6},{5,7},{6,0},{7,1},{8,10},{9,11},{10,... | collective-permute-start | bytes 1179656 | tf_op jit(solution)/shard_map/ppermute | solution.py:382
  165.6 12.9 %collective-permute-start.34 = (bf16[96,2048]{1,0:T(8,128)(2,1)S(1)}, bf16[96,2048]{1,0:T(8,128)(2,1)S(1)}, u32[]{:S(2)}, u32[]{:S(2)}) collective-permute-start(bf16[96,2048]{1,0:T(8,128)(2,1)S(1)} %get-tuple-element.117), channel_id=1, source_target_pairs={{0,6},{1,7},{2,0},{3,1},{4,2},{5,3},{6,4},{7,5},{8,14},{9,15},{10,... | collective-permute-start | bytes 1179656 | tf_op jit(solution)/shard_map/ppermute | solution.py:382
  168.9 18.0 %collective-permute-start.38 = (bf16[96,2048]{1,0:T(8,128)(2,1)S(1)}, bf16[96,2048]{1,0:T(8,128)(2,1)S(1)}, u32[]{:S(2)}, u32[]{:S(2)}) collective-permute-start(bf16[96,2048]{1,0:T(8,128)(2,1)S(1)} %get-tuple-element.122), channel_id=1, source_target_pairs={{0,6},{1,7},{2,0},{3,1},{4,2},{5,3},{6,4},{7,5},{8,14},{9,15},{10,... | collective-permute-start | bytes 1179656 | tf_op jit(solution)/shard_map/ppermute | solution.py:382
  168.9 22.8 %collective-permute-start.42 = (bf16[96,2048]{1,0:T(8,128)(2,1)S(1)}, bf16[96,2048]{1,0:T(8,128)(2,1)S(1)}, u32[]{:S(2)}, u32[]{:S(2)}) collective-permute-start(bf16[96,2048]{1,0:T(8,128)(2,1)S(1)} %get-tuple-element.126), channel_id=1, source_target_pairs={{0,2},{1,3},{2,4},{3,5},{4,6},{5,7},{6,0},{7,1},{8,10},{9,11},{10,... | collective-permute-start | bytes 1179656 | tf_op jit(solution)/shard_map/ppermute | solution.py:382
  174.8 16.7 %collective-permute-start.40 = (bf16[96,2048]{1,0:T(8,128)(2,1)S(1)}, bf16[96,2048]{1,0:T(8,128)(2,1)S(1)}, u32[]{:S(2)}, u32[]{:S(2)}) collective-permute-start(bf16[96,2048]{1,0:T(8,128)(2,1)S(1)} %add.269), channel_id=1, source_target_pairs={{0,2},{1,3},{2,4},{3,5},{4,6},{5,7},{6,0},{7,1},{8,10},{9,11},{10,... | collective-permute-start | bytes 1179656 | tf_op jit(solution)/shard_map/ppermute | solution.py:382
  178.5 21.0 %collective-permute-start.43 = (bf16[96,2048]{1,0:T(8,128)(2,1)S(1)}, bf16[96,2048]{1,0:T(8,128)(2,1)S(1)}, u32[]{:S(2)}, u32[]{:S(2)}) collective-permute-start(bf16[96,2048]{1,0:T(8,128)(2,1)S(1)} %add.273), channel_id=1, source_target_pairs={{0,6},{1,7},{2,0},{3,1},{4,2},{5,3},{6,4},{7,5},{8,14},{9,15},{10,... | collective-permute-start | bytes 1179656 | tf_op jit(solution)/shard_map/ppermute | solution.py:382
  182.4 19.4 %collective-permute-start.35 = (bf16[48,2048]{1,0:T(8,128)(2,1)S(1)}, bf16[48,2048]{1,0:T(8,128)(2,1)S(1)}, u32[]{:S(2)}, u32[]{:S(2)}) collective-permute-start(bf16[48,2048]{1,0:T(8,128)(2,1)S(1)} %get-tuple-element.135), channel_id=1, source_target_pairs={{0,2},{1,3},{2,4},{3,5},{4,6},{5,7},{6,0},{7,1},{8,10},{9,11},{10,... | collective-permute-start | bytes 589832 | tf_op jit(solution)/shard_map/ppermute | solution.py:382
  186.8 15.0 %collective-permute-start.37 = (bf16[48,2048]{1,0:T(8,128)(2,1)S(1)}, bf16[48,2048]{1,0:T(8,128)(2,1)S(1)}, u32[]{:S(2)}, u32[]{:S(2)}) collective-permute-start(bf16[48,2048]{1,0:T(8,128)(2,1)S(1)} %get-tuple-element.136), channel_id=1, source_target_pairs={{0,4},{1,5},{2,6},{3,7},{4,0},{5,1},{6,2},{7,3},{8,12},{9,13},{10,... | collective-permute-start | bytes 589832 | tf_op jit(solution)/shard_map/ppermute | solution.py:382
  191.5 10.7 %collective-permute-start.36 = (bf16[48,2048]{1,0:T(8,128)(2,1)S(1)}, bf16[48,2048]{1,0:T(8,128)(2,1)S(1)}, u32[]{:S(2)}, u32[]{:S(2)}) collective-permute-start(bf16[48,2048]{1,0:T(8,128)(2,1)S(1)} %get-tuple-element.137), channel_id=1, source_target_pairs={{0,6},{1,7},{2,0},{3,1},{4,2},{5,3},{6,4},{7,5},{8,14},{9,15},{10,... | collective-permute-start | bytes 589832 | tf_op jit(solution)/shard_map/ppermute | solution.py:382
  191.7 10.7 %collective-permute-start.41 = (bf16[48,2048]{1,0:T(8,128)(2,1)S(1)}, bf16[48,2048]{1,0:T(8,128)(2,1)S(1)}, u32[]{:S(2)}, u32[]{:S(2)}) collective-permute-start(bf16[48,2048]{1,0:T(8,128)(2,1)S(1)} %slice.108), channel_id=1, source_target_pairs={{0,1},{1,0},{2,3},{3,2},{4,5},{5,4},{6,7},{7,6},{8,9},{9,8},{10,11... | collective-permute-start | bytes 589832 | tf_op jit(solution)/shard_map/ppermute | solution.py:385
  199.7 7.3 %collective-permute-start.44 = (bf16[48,2048]{1,0:T(8,128)(2,1)S(1)}, bf16[48,2048]{1,0:T(8,128)(2,1)S(1)}, u32[]{:S(2)}, u32[]{:S(2)}) collective-permute-start(bf16[48,2048]{1,0:T(8,128)(2,1)S(1)} %slice.107), channel_id=1, source_target_pairs={{0,1},{1,0},{2,3},{3,2},{4,5},{5,4},{6,7},{7,6},{8,9},{9,8},{10,11... | collective-permute-start | bytes 589832 | tf_op jit(solution)/shard_map/ppermute | solution.py:385
where the time goes:
time: 208 us
  Pallas kernels  69.3 us (33%)
  waiting for transfers between devices  67.2 us (32%)
  starting transfers between devices  62.2 us (30%)
  local copies, waits for them, and re-layouts  5.41 us (3%)
  other arithmetic  2.52 us (1%)
    ppermute x18, waiting for transfers between devices, along_z(): lax.ppermute(x, 'head', [(i, (i + 2 * k) % shards) for i in range(shards)])  29.9 us
    pallas_call x3, Pallas kernels, backward(): pl.pallas_call(kernel, out_shape=(head, *tail), scratch_shapes=[pltpu.VME...  28 us
    ppermute x18, starting transfers between devices, along_z(): lax.ppermute(x, 'head', [(i, (i + 2 * k) % shards) for i in range(shards)])  25.7 us
    ppermute x15, waiting for transfers between devices, along_y(): lax.ppermute(x, 'slab', [(i, (i + 4 * k) % slabs) for i in range(slabs)])  25.4 us
    ppermute x15, starting transfers between devices, along_y(): lax.ppermute(x, 'slab', [(i, (i + 4 * k) % slabs) for i in range(slabs)])  20.8 us
    pallas_call x1, Pallas kernels, forward(): pl.pallas_call(functools.partial(forward_kernel, scale2), out_shape=(jax....  14.8 us
    pallas_call x3, Pallas kernels, project(): pl.pallas_call(functools.partial(project_kernel, len(blocks), height, acc...  13.1 us
    ppermute x6, starting transfers between devices, across_far(): return lax.ppermute(x, 'head', [(i, i ^ 1) for i in range(shards)])  12.9 us
  transfers between devices with their start and end apart: 45, of which 24 were waited for; matrix products, arithmetic and copies ran while one was open for 2% of the time, Pallas kernels for 20%

commit v1 on v0

--- a/solution.py
+++ b/solution.py
@@ -409,7 +409,7 @@
     b = after(b, far_a, up_c)
     pair_b = jnp.concatenate([b, across_far(b)])
     down_b = along_z(pair_b, -1)
-    up_b = along_z(after(pair_b, up_a), 1)
+    up_b = along_z(after(pair_b, far_c), 1)
     two_a, two_b = along_z(up_a, 1), along_z(down_b, -1)
     grads = [out_grad, along_y(after(out_grad, up_c), 1)]
     grads.append(along_y(after(out_grad, grads[1]), -1))

time: 208 us -> 205 us (0.986)
  waiting for transfers between devices: 67.2 us -> 64 us
    ppermute x6, waiting for transfers between devices: 7.16 us -> 3.15 us  [across_far(): return lax.ppermute(x, 'head', [(i, i ^ 1) for i in range(shards)])]
    ppermute x15, starting transfers between devices: 20.8 us -> 18.4 us  [along_y(): lax.ppermute(x, 'slab', [(i, (i + 4 * k) % slabs) for i in range(slabs)])]
  transfers between devices with their start and end apart: 45 -> 45, of which waited for: 24 -> 25; matrix products, arithmetic and copies ran while one was open for 2% -> 2% of each run, Pallas kernels for 20% -> 21%
where the time goes in v1:
time: 205 us; the launch traced here: 203 us
  Pallas kernels  69.3 us (34%)
  waiting for transfers between devices  64 us (31%)
  starting transfers between devices  60.8 us (30%)
  local copies, waits for them, and re-layouts  5.41 us (3%)
  other arithmetic  2.53 us (1%)
    ppermute x18, waiting for transfers between devices, along_z(): lax.ppermute(x, 'head', [(i, (i + 2 * k) % shards) for i in range(shards)])  29.6 us
    pallas_call x3, Pallas kernels, backward(): pl.pallas_call(kernel, out_shape=(head, *tail), scratch_shapes=[pltpu.VME...  28 us
    ppermute x18, starting transfers between devices, along_z(): lax.ppermute(x, 'head', [(i, (i + 2 * k) % shards) for i in range(shards)])  26.8 us
    ppermute x15, waiting for transfers between devices, along_y(): lax.ppermute(x, 'slab', [(i, (i + 4 * k) % slabs) for i in range(slabs)])  26.6 us
    ppermute x15, starting transfers between devices, along_y(): lax.ppermute(x, 'slab', [(i, (i + 4 * k) % slabs) for i in range(slabs)])  18.4 us
    pallas_call x1, Pallas kernels, forward(): pl.pallas_call(functools.partial(forward_kernel, scale2), out_shape=(jax....  14.8 us
    ppermute x6, starting transfers between devices, across_far(): return lax.ppermute(x, 'head', [(i, i ^ 1) for i in range(shards)])  13.5 us
    pallas_call x3, Pallas kernels, project(): pl.pallas_call(functools.partial(project_kernel, len(blocks), height, acc...  13.1 us
  transfers between devices with their start and end apart: 45, of which 25 were waited for; matrix products, arithmetic and copies ran while one was open for 2% of the time, Pallas kernels for 21%

profile of v1, /device:TPU:0, one launch (start us, length us, event | category | flops | bytes accessed | tf_op | source)
XLA Modules:
  0.0 203.2 jit_solution(5071310946557955920)
XLA Ops:
  0.6 1.2 fusion.9
  1.8 4.0 %collective-permute-start.4 = (bf16[48,2048]{1,0:T(8,128)(2,1)S(1)}, bf16[48,2048]{1,0:T(8,128)(2,1)S(1)}, u32[]{:S(2)}, u32[]{:S(2)}) collective-permute-start(bf16[48,2048]{1,0:T(8,128)(2,1)S(1)} %get-tuple-element.138), channel_id=1, source_target_pairs={{0,4},{1,5},{2,6},{3,7},{4,0},{5,1},{6,2},{7,3},{8,12},{9,13},{10,... | collective-permute-start | bytes 589832 | tf_op jit(solution)/shard_map/ppermute | solution.py:382
  6.6 1.3 collective-permute-start.1
  7.9 3.0 %collective-permute-start = (bf16[48,2048]{1,0:T(8,128)(2,1)S(1)}, bf16[48,2048]{1,0:T(8,128)(2,1)S(1)}, u32[]{:S(2)}, u32[]{:S(2)}) collective-permute-start(bf16[48,2048]{1,0:T(8,128)(2,1)S(1)} %get-tuple-element.140), channel_id=1, source_target_pairs={{0,1},{1,0},{2,3},{3,2},{4,5},{5,4},{6,7},{7,6},{8,9},{9,8},{10,11... | collective-permute-start | bytes 589832 | tf_op jit(solution)/shard_map/ppermute | solution.py:385
  11.1 3.9 %collective-permute-done.1 = bf16[48,2048]{1,0:T(8,128)(2,1)S(1)} collective-permute-done((bf16[48,2048]{1,0:T(8,128)(2,1)S(1)}, bf16[48,2048]{1,0:T(8,128)(2,1)S(1)}, u32[]{:S(2)}, u32[]{:S(2)}) %collective-permute-start.1) | collective-permute-done | bytes 196640 | tf_op jit(solution)/shard_map/ppermute | solution.py:382
  15.2 3.0 %collective-permute-start.2 = (bf16[48,2048]{1,0:T(8,128)(2,1)S(1)}, bf16[48,2048]{1,0:T(8,128)(2,1)S(1)}, u32[]{:S(2)}, u32[]{:S(2)}) collective-permute-start(bf16[48,2048]{1,0:T(8,128)(2,1)S(1)} %get-tuple-element.65), channel_id=1, source_target_pairs={{0,1},{1,0},{2,3},{3,2},{4,5},{5,4},{6,7},{7,6},{8,9},{9,8},{10,11... | collective-permute-start | bytes 589832 | tf_op jit(solution)/shard_map/ppermute | solution.py:385
  18.2 1.6 collective-permute-start.12
  20.5 1.6 collective-permute-start.9
  22.1 1.4 collective-permute-done.2
  23.6 1.6 collective-permute-start.7
  25.1 2.3 %collective-permute-done.12.g1.refs_5_.refs_3_ = bf16[384,384]{1,0:T(8,128)(2,1)S(1)} collective-permute-done((bf16[384,384]{1,0:T(8,128)(2,1)}, bf16[384,384]{1,0:T(8,128)(2,1)S(1)}, u32[]{:S(2)}, u32[]{:S(2)}) %collective-permute-start.12) | collective-permute-done | bytes 294944 | tf_op jit(solution)/shard_map/ppermute | solution.py:373
  28.2 1.7 collective-permute-start.13
  30.3 0.9 broadcast_in_dim.17
  31.3 1.9 reshape.18
  33.2 2.0 collective-permute-start.10
  35.3 3.2 %collective-permute-start.8 = (bf16[96,2048]{1,0:T(8,128)(2,1)S(1)}, bf16[96,2048]{1,0:T(8,128)(2,1)S(1)}, u32[]{:S(2)}, u32[]{:S(2)}) collective-permute-start(bf16[96,2048]{1,0:T(8,128)(2,1)S(1)} %collective-permute-done.7.refs_2_), channel_id=1, source_target_pairs={{0,6},{1,7},{2,0},{3,1},{4,2},{5,3},{6,4},{7,5},{8,14},{9,15},{10,... | collective-permute-start | bytes 1179656 | tf_op jit(solution)/shard_map/ppermute | solution.py:382
  39.6 1.4 collective-permute-start.6
  41.0 5.1 %project.3.refs_5_ = f32[3,384,384]{2,1,0:T(8,128)S(1)} custom-call(s32[8]{0:T(128)S(1)} %stack.50.place, bf16[192,2048]{1,0:T(8,128)(2,1)S(1)} %pad_maximum_fusion.refs_0_, bf16[192,2048]{1,0:T(8,128)(2,1)} %collective-permute-done.5.refs_1_, bf16[3,6144,384]{2,1,0:T(8,128)(2,1)} %w_ref.5), custom_call_target="tpu_custom_call" | custom-call | flops 6899999744 | tf_op jit(solution)/shard_map/project/pallas_call | solution.py:91
  46.1 2.6 %collective-permute-done.11.refs_3_ = bf16[96,2048]{1,0:T(8,128)(2,1)S(1)} collective-permute-done((bf16[96,2048]{1,0:T(8,128)(2,1)}, bf16[96,2048]{1,0:T(8,128)(2,1)S(1)}, u32[]{:S(2)}, u32[]{:S(2)}) %collective-permute-start.11) | collective-permute-done | bytes 393248 | tf_op jit(solution)/shard_map/ppermute | solution.py:382
  48.7 4.2 %project.4.refs_5_ = f32[3,384,384]{2,1,0:T(8,128)S(1)} custom-call(s32[8]{0:T(128)S(1)} %stack.49.place, bf16[96,2048]{1,0:T(8,128)(2,1)S(1)} %pad_maximum_fusion.2.refs_0_, bf16[96,2048]{1,0:T(8,128)(2,1)} %collective-permute-done.9.refs_1_, bf16[96,2048]{1,0:T(8,128)(2,1)S(1)} %collective-permute-done.10.refs_2_, ...), custom_call_target="tpu_custom_call" | custom-call | flops 6899999744 | tf_op jit(solution)/shard_map/project/pallas_call | solution.py:91
  52.9 1.1 collective-permute-done.6.refs_1_
  54.0 3.8 %project.5 = (bf16[384,384]{1,0:T(8,128)(2,1)S(1)}, bf16[384,768]{1,0:T(8,128)(2,1)S(1)}) custom-call(s32[8]{0:T(128)S(1)} %stack.49.place, bf16[96,2048]{1,0:T(8,128)(2,1)S(1)} %constant_dynamic-update-slice_fusion.refs_0_, bf16[96,2048]{1,0:T(8,128)(2,1)S(1)} %collective-permute-done.6.refs_1_, bf16[96,2048]{1,0:T(8,128)(2,1)S(1)} %collective-permute-done.7.refs_2_, ...), custom_call_target="tpu_custom_call" | custom-call | flops 6899999744 | tf_op jit(solution)/shard_map/project/pallas_call | solution.py:91
  57.9 1.0 collective-permute-start.15
  59.5 2.0 collective-permute-start.17
  61.5 7.8 %collective-permute-done.18.q3.refs_3_.refs_2_ = bf16[384,384]{1,0:T(8,128)(2,1)S(1)} collective-permute-done((bf16[384,384]{1,0:T(8,128)(2,1)S(1)}, bf16[384,384]{1,0:T(8,128)(2,1)S(1)}, u32[]{:S(2)}, u32[]{:S(2)}) %collective-permute-start.18) | collective-permute-done | bytes 294944 | tf_op jit(solution)/shard_map/ppermute | solution.py:373
  69.3 2.6 %collective-permute-done.17.q2.refs_2_.refs_1_ = bf16[384,384]{1,0:T(8,128)(2,1)S(1)} collective-permute-done((bf16[384,384]{1,0:T(8,128)(2,1)S(1)}, bf16[384,384]{1,0:T(8,128)(2,1)S(1)}, u32[]{:S(2)}, u32[]{:S(2)}) %collective-permute-start.17) | collective-permute-done | bytes 294944 | tf_op jit(solution)/shard_map/ppermute | solution.py:373
  72.7 2.0 collective-permute-done.19.kv3.refs_9_
  74.6 14.8 %forward.1 = (bf16[4,3,128,384]{3,2,1,0:T(8,128)(2,1)S(1)}, f32[4,9,384]{2,1,0:T(8,128)S(1)}) custom-call(bf16[384,384]{1,0:T(8,128)(2,1)S(1)} %get-tuple-element.72.q0.refs_0_, bf16[384,384]{1,0:T(8,128)(2,1)S(1)} %collective-permute-done.16.q1.refs_1_.refs_0_, bf16[384,384]{1,0:T(8,128)(2,1)S(1)} %collective-permute-done.17.q2.refs_2_.refs_1_, ...), custom_call_target="tpu_custom_call" | custom-call | flops 19549999104 | tf_op jit(solution)/shard_map/forward/pallas_call | solution.py:150
  89.5 2.1 %collective-permute-start.23 = (f32[4,9,384]{2,1,0:T(8,128)S(1)}, f32[4,9,384]{2,1,0:T(8,128)S(1)}, u32[]{:S(2)}, u32[]{:S(2)}) collective-permute-start(f32[4,9,384]{2,1,0:T(8,128)S(1)} %get-tuple-element.82.s0), channel_id=1, source_target_pairs={{0,64},{8,72},{16,80},{24,88},{32,96},{40,104},{48,112},{56,120},{... | collective-permute-start | bytes 165896 | tf_op jit(solution)/shard_map/ppermute | solution.py:373
  91.6 1.7 collective-permute-start.22
  93.6 3.0 %collective-permute-done.23.s3 = f32[4,9,384]{2,1,0:T(8,128)S(1)} collective-permute-done((f32[4,9,384]{2,1,0:T(8,128)S(1)}, f32[4,9,384]{2,1,0:T(8,128)S(1)}, u32[]{:S(2)}, u32[]{:S(2)}) %collective-permute-start.23) | collective-permute-done | bytes 55328 | tf_op jit(solution)/shard_map/ppermute | solution.py:373
  97.3 1.8 collective-permute-done.21.s1
  99.3 1.0 collective-permute-start.26
  100.3 1.7 collective-permute-start.25
  102.3 12.8 %backward.3 = (f32[4,3,128,384]{3,2,1,0:T(8,128)S(1)}, bf16[384,768]{1,0:T(8,128)(2,1)S(1)}, bf16[384,768]{1,0:T(8,128)(2,1)S(1)}) custom-call(bf16[384,384]{1,0:T(8,128)(2,1)S(1)} %get-tuple-element.72.q0.refs_0_, bf16[384,384]{1,0:T(8,128)(2,1)S(1)} %collective-permute-done.16.q1.refs_1_.refs_0_, ...), custom_call_target="tpu_custom_call" | custom-call | flops 18400000000 | tf_op jit(solution)/shard_map/backward/pallas_call | solution.py:300
  115.3 1.1 merge.1
  116.3 0.9 collective-permute-done.27
  117.4 1.0 collective-permute-start.28
  118.4 10.6 %backward.4 = (bf16[3,384,384]{2,1,0:T(8,128)(2,1)S(1)}, f32[768,384]{1,0:T(8,128)S(1)}, f32[768,384]{1,0:T(8,128)S(1)}) custom-call(bf16[384,384]{1,0:T(8,128)(2,1)S(1)} %collective-permute-done.16.q1.refs_1_.refs_0_, bf16[384,384]{1,0:T(8,128)(2,1)S(1)} %collective-permute-done.17.q2.refs_2_.refs_1_, ...), custom_call_target="tpu_custom_call" | custom-call | flops 13799999488 | tf_op jit(solution)/shard_map/backward/pallas_call | solution.py:300
  129.1 2.7 %collective-permute-start.31 = (bf16[384,384]{1,0:T(8,128)(2,1)S(1)}, bf16[384,384]{1,0:T(8,128)(2,1)S(1)}, u32[]{:S(2)}, u32[]{:S(2)}) collective-permute-start(bf16[384,384]{1,0:T(8,128)(2,1)S(1)} %get-tuple-element.132), channel_id=1, source_target_pairs={{0,64},{8,72},{16,80},{24,88},{32,96},{40,104},{48,112},{56,120},{... | collective-permute-start | bytes 884744 | tf_op jit(solution)/shard_map/ppermute | solution.py:373
  131.8 1.6 collective-permute-start.30
  133.8 4.6 %backward.5 = (bf16[1,384,384]{2,1,0:T(8,128)(2,1)S(1)}, bf16[384,768]{1,0:T(8,128)(2,1)S(1)}, bf16[384,768]{1,0:T(8,128)(2,1)S(1)}) custom-call(bf16[384,384]{1,0:T(8,128)(2,1)S(1)} %get-tuple-element.72.q0.refs_0_, bf16[384,384]{1,0:T(8,128)(2,1)} %refs_1_.1, bf16[384,768]{1,0:T(8,128)(2,1)S(1)} %get-tuple-element.73.kv0.refs_6_.refs_2_, ...), custom_call_target="tpu_custom_call" | custom-call | flops 4600000000 | tf_op jit(solution)/shard_map/backward/pallas_call | solution.py:300
  138.4 2.2 %collective-permute-done.31 = bf16[384,384]{1,0:T(8,128)(2,1)S(1)} collective-permute-done((bf16[384,384]{1,0:T(8,128)(2,1)S(1)}, bf16[384,384]{1,0:T(8,128)(2,1)S(1)}, u32[]{:S(2)}, u32[]{:S(2)}) %collective-permute-start.31) | collective-permute-done | bytes 294944 | tf_op jit(solution)/shard_map/ppermute | solution.py:373
  140.6 5.5 %collective-permute-done.30 = bf16[384,384]{1,0:T(8,128)(2,1)S(1)} collective-permute-done((bf16[384,384]{1,0:T(8,128)(2,1)S(1)}, bf16[384,384]{1,0:T(8,128)(2,1)S(1)}, u32[]{:S(2)}, u32[]{:S(2)}) %collective-permute-start.30) | collective-permute-done | bytes 294944 | tf_op jit(solution)/shard_map/ppermute | solution.py:373
  146.3 1.8 collective-permute-done.32
  148.3 4.1 %spread.3 = (bf16[96,2048]{1,0:T(8,128)(2,1)S(1)}, bf16[96,2048]{1,0:T(8,128)(2,1)S(1)}, bf16[96,2048]{1,0:T(8,128)(2,1)S(1)}, bf16[96,2048]{1,0:T(8,128)(2,1)S(1)}) custom-call(s32[8]{0:T(128)S(1)} %stack.49.place, bf16[384,384]{1,0:T(8,128)(2,1)S(1)} %fusion.2.dq, bf16[384,768]{1,0:T(8,128)(2,1)S(1)} %add_convert_fusion.dkv, bf16[3,6144,384]{2,1,0:T(8,128)(2,1)S(1)} %bitcast.36), custom_call_target="tpu_custom_call" | custom-call | flops 345000000 | tf_op jit(solution)/shard_map/spread/pallas_call | solution.py:340
  152.4 4.1 %spread.4 = (bf16[48,2048]{1,0:T(8,128)(2,1)S(1)}, bf16[48,2048]{1,0:T(8,128)(2,1)S(1)}, bf16[48,2048]{1,0:T(8,128)(2,1)S(1)}, bf16[48,2048]{1,0:T(8,128)(2,1)S(1)}, bf16[192,2048]{1,0:T(8,128)(2,1)S(1)}) custom-call(s32[8]{0:T(128)S(1)} %stack.50.place, bf16[384,384]{1,0:T(8,128)(2,1)S(1)} %fusion.2.dq, bf16[384,768]{1,0:T(8,128)(2,1)S(1)} %add_convert_fusion.dkv, ...), custom_call_target="tpu_custom_call" | custom-call | flops 345000000 | tf_op jit(solution)/shard_map/spread/pallas_call | solution.py:340
  156.5 1.9 collective-permute-start.33
  158.4 2.7 %collective-permute-start.39 = (bf16[96,2048]{1,0:T(8,128)(2,1)S(1)}, bf16[96,2048]{1,0:T(8,128)(2,1)S(1)}, u32[]{:S(2)}, u32[]{:S(2)}) collective-permute-start(bf16[96,2048]{1,0:T(8,128)(2,1)S(1)} %get-tuple-element.124), channel_id=1, source_target_pairs={{0,2},{1,3},{2,4},{3,5},{4,6},{5,7},{6,0},{7,1},{8,10},{9,11},{10,... | collective-permute-start | bytes 1179656 | tf_op jit(solution)/shard_map/ppermute | solution.py:382
  161.1 4.1 %spread.5 = (bf16[96,2048]{1,0:T(8,128)(2,1)S(1)}, bf16[96,2048]{1,0:T(8,128)(2,1)S(1)}, bf16[96,2048]{1,0:T(8,128)(2,1)S(1)}, bf16[96,2048]{1,0:T(8,128)(2,1)S(1)}) custom-call(s32[8]{0:T(128)S(1)} %stack.49.place, bf16[384,384]{1,0:T(8,128)(2,1)S(1)} %fusion.2.dq, bf16[384,768]{1,0:T(8,128)(2,1)S(1)} %add_convert_fusion.dkv, bf16[3,6144,384]{2,1,0:T(8,128)(2,1)S(1)} %bitcast.36), custom_call_target="tpu_custom_call" | custom-call | flops 345000000 | tf_op jit(solution)/shard_map/spread/pallas_call | solution.py:340
  166.6 1.2 collective-permute-start.42
  167.8 3.7 %collective-permute-done.39 = bf16[96,2048]{1,0:T(8,128)(2,1)S(1)} collective-permute-done((bf16[96,2048]{1,0:T(8,128)(2,1)S(1)}, bf16[96,2048]{1,0:T(8,128)(2,1)S(1)}, u32[]{:S(2)}, u32[]{:S(2)}) %collective-permute-start.39) | collective-permute-done | bytes 393248 | tf_op jit(solution)/shard_map/ppermute | solution.py:382
  171.5 1.7 collective-permute-start.40
  173.3 4.0 %collective-permute-done.34 = bf16[96,2048]{1,0:T(8,128)(2,1)S(1)} collective-permute-done((bf16[96,2048]{1,0:T(8,128)(2,1)S(1)}, bf16[96,2048]{1,0:T(8,128)(2,1)S(1)}, u32[]{:S(2)}, u32[]{:S(2)}) %collective-permute-start.34) | collective-permute-done | bytes 393248 | tf_op jit(solution)/shard_map/ppermute | solution.py:382
  177.4 1.8 collective-permute-start.43
  179.7 6.0 %collective-permute-done.38 = bf16[96,2048]{1,0:T(8,128)(2,1)S(1)} collective-permute-done((bf16[96,2048]{1,0:T(8,128)(2,1)S(1)}, bf16[96,2048]{1,0:T(8,128)(2,1)S(1)}, u32[]{:S(2)}, u32[]{:S(2)}) %collective-permute-start.38) | collective-permute-done | bytes 393248 | tf_op jit(solution)/shard_map/ppermute | solution.py:382
  186.5 1.8 collective-permute-done.40
  188.3 0.9 collective-permute-start.36
  189.4 1.9 collective-permute-start.41
  191.3 3.6 %collective-permute-done.43 = bf16[96,2048]{1,0:T(8,128)(2,1)S(1)} collective-permute-done((bf16[96,2048]{1,0:T(8,128)(2,1)S(1)}, bf16[96,2048]{1,0:T(8,128)(2,1)S(1)}, u32[]{:S(2)}, u32[]{:S(2)}) %collective-permute-start.43) | collective-permute-done | bytes 393248 | tf_op jit(solution)/shard_map/ppermute | solution.py:382
  195.1 3.2 %collective-permute-start.44 = (bf16[48,2048]{1,0:T(8,128)(2,1)S(1)}, bf16[48,2048]{1,0:T(8,128)(2,1)S(1)}, u32[]{:S(2)}, u32[]{:S(2)}) collective-permute-start(bf16[48,2048]{1,0:T(8,128)(2,1)S(1)} %slice.107), channel_id=1, source_target_pairs={{0,1},{1,0},{2,3},{3,2},{4,5},{5,4},{6,7},{7,6},{8,9},{9,8},{10,11... | collective-permute-start | bytes 589832 | tf_op jit(solution)/shard_map/ppermute | solution.py:385
  198.2 2.9 %collective-permute-done.36 = bf16[48,2048]{1,0:T(8,128)(2,1)S(1)} collective-permute-done((bf16[48,2048]{1,0:T(8,128)(2,1)S(1)}, bf16[48,2048]{1,0:T(8,128)(2,1)S(1)}, u32[]{:S(2)}, u32[]{:S(2)}) %collective-permute-start.36) | collective-permute-done | bytes 196640 | tf_op jit(solution)/shard_map/ppermute | solution.py:382
  201.4 0.9 collective-permute-done.44
  202.4 0.9 pad_maximum_fusion.1
  (90 shorter events, 11.6 us)
Async XLA Ops:
  0.6 10.3 %copy-start.4 = (s32[48]{0:T(128)S(1)}, s32[48]{0:T(128)}, u32[]{:S(2)}) copy-start(s32[48]{0:T(128)} %param.8) | copy-start | bytes 580
  1.8 18.0 %collective-permute-start.4 = (bf16[48,2048]{1,0:T(8,128)(2,1)S(1)}, bf16[48,2048]{1,0:T(8,128)(2,1)S(1)}, u32[]{:S(2)}, u32[]{:S(2)}) collective-permute-start(bf16[48,2048]{1,0:T(8,128)(2,1)S(1)} %get-tuple-element.138), channel_id=1, source_target_pairs={{0,4},{1,5},{2,6},{3,7},{4,0},{5,1},{6,2},{7,3},{8,12},{9,13},{10,... | collective-permute-start | bytes 589832 | tf_op jit(solution)/shard_map/ppermute | solution.py:382
  5.8 13.9 %collective-permute-start.3 = (bf16[48,2048]{1,0:T(8,128)(2,1)S(1)}, bf16[48,2048]{1,0:T(8,128)(2,1)S(1)}, u32[]{:S(2)}, u32[]{:S(2)}) collective-permute-start(bf16[48,2048]{1,0:T(8,128)(2,1)S(1)} %get-tuple-element.138), channel_id=1, source_target_pairs={{0,6},{1,7},{2,0},{3,1},{4,2},{5,3},{6,4},{7,5},{8,14},{9,15},{10,... | collective-permute-start | bytes 589832 | tf_op jit(solution)/shard_map/ppermute | solution.py:382
  6.6 8.4 %collective-permute-start.1 = (bf16[48,2048]{1,0:T(8,128)(2,1)S(1)}, bf16[48,2048]{1,0:T(8,128)(2,1)S(1)}, u32[]{:S(2)}, u32[]{:S(2)}) collective-permute-start(bf16[48,2048]{1,0:T(8,128)(2,1)S(1)} %get-tuple-element.138), channel_id=1, source_target_pairs={{0,2},{1,3},{2,4},{3,5},{4,6},{5,7},{6,0},{7,1},{8,10},{9,11},{10,... | collective-permute-start | bytes 589832 | tf_op jit(solution)/shard_map/ppermute | solution.py:382
  7.9 7.3 %collective-permute-start = (bf16[48,2048]{1,0:T(8,128)(2,1)S(1)}, bf16[48,2048]{1,0:T(8,128)(2,1)S(1)}, u32[]{:S(2)}, u32[]{:S(2)}) collective-permute-start(bf16[48,2048]{1,0:T(8,128)(2,1)S(1)} %get-tuple-element.140), channel_id=1, source_target_pairs={{0,1},{1,0},{2,3},{3,2},{4,5},{5,4},{6,7},{7,6},{8,9},{9,8},{10,11... | collective-permute-start | bytes 589832 | tf_op jit(solution)/shard_map/ppermute | solution.py:385
  15.2 8.4 %collective-permute-start.2 = (bf16[48,2048]{1,0:T(8,128)(2,1)S(1)}, bf16[48,2048]{1,0:T(8,128)(2,1)S(1)}, u32[]{:S(2)}, u32[]{:S(2)}) collective-permute-start(bf16[48,2048]{1,0:T(8,128)(2,1)S(1)} %get-tuple-element.65), channel_id=1, source_target_pairs={{0,1},{1,0},{2,3},{3,2},{4,5},{5,4},{6,7},{7,6},{8,9},{9,8},{10,11... | collective-permute-start | bytes 589832 | tf_op jit(solution)/shard_map/ppermute | solution.py:385
  18.2 9.2 %collective-permute-start.12 = (bf16[384,384]{1,0:T(8,128)(2,1)}, bf16[384,384]{1,0:T(8,128)(2,1)S(1)}, u32[]{:S(2)}, u32[]{:S(2)}) collective-permute-start(bf16[384,384]{1,0:T(8,128)(2,1)} %refs_1_.1), channel_id=1, source_target_pairs={{0,32},{8,40},{16,48},{24,56},{32,64},{40,72},{48,80},{56,88},{64,... | collective-permute-start | bytes 884744 | tf_op jit(solution)/shard_map/ppermute | solution.py:373
  19.9 10.4 %copy-start.3 = (s32[3]{0:T(128)S(1)}, s32[3]{0:T(128)}, u32[]{:S(2)}) copy-start(s32[3]{0:T(128)} %param.9) | copy-start | bytes 40
  19.9 19.7 %collective-permute-start.5 = (bf16[192,2048]{1,0:T(8,128)(2,1)S(1)}, bf16[192,2048]{1,0:T(8,128)(2,1)}, u32[]{:S(2)}, u32[]{:S(2)}) collective-permute-start(bf16[192,2048]{1,0:T(8,128)(2,1)S(1)} %pad_maximum_fusion.refs_0_), channel_id=1, source_target_pairs={{0,1},{1,0},{2,3},{3,2},{4,5},{5,4},{6,7},{7,6},{8,9},{9,8},{10,11... | collective-permute-start | bytes 2359304 | tf_op jit(solution)/shard_map/ppermute | solution.py:385
  20.5 14.7 %collective-permute-start.9 = (bf16[96,2048]{1,0:T(8,128)(2,1)S(1)}, bf16[96,2048]{1,0:T(8,128)(2,1)}, u32[]{:S(2)}, u32[]{:S(2)}) collective-permute-start(bf16[96,2048]{1,0:T(8,128)(2,1)S(1)} %pad_maximum_fusion.2.refs_0_), channel_id=1, source_target_pairs={{0,2},{1,3},{2,4},{3,5},{4,6},{5,7},{6,0},{7,1},{8,10},{9,11},{10,... | collective-permute-start | bytes 1179656 | tf_op jit(solution)/shard_map/ppermute | solution.py:382
  23.6 11.7 %collective-permute-start.7 = (bf16[96,2048]{1,0:T(8,128)(2,1)S(1)}, bf16[96,2048]{1,0:T(8,128)(2,1)S(1)}, u32[]{:S(2)}, u32[]{:S(2)}) collective-permute-start(bf16[96,2048]{1,0:T(8,128)(2,1)S(1)} %constant_dynamic-update-slice_fusion.refs_0_), channel_id=1, source_target_pairs={{0,6},{1,7},{2,0},{3,1},{4,2},{5,3},{6,4},{7,5},{8,14},{9,15},{10,... | collective-permute-start | bytes 1179656 | tf_op jit(solution)/shard_map/ppermute | solution.py:382
  27.4 0.7 copy-start
  28.2 10.3 %collective-permute-start.13 = (bf16[384,384]{1,0:T(8,128)(2,1)}, bf16[384,384]{1,0:T(8,128)(2,1)}, u32[]{:S(2)}, u32[]{:S(2)}) collective-permute-start(bf16[384,384]{1,0:T(8,128)(2,1)} %refs_1_.1), channel_id=1, source_target_pairs={{0,96},{8,104},{16,112},{24,120},{32,0},{40,8},{48,16},{56,24},{64... | collective-permute-start | bytes 884744 | tf_op jit(solution)/shard_map/ppermute | solution.py:373
  31.3 17.4 %slice-start = ((s8[14155776]{0:T(1024)(128)(4,1)}), s8[1572864]{0:T(1024)(128)(4,1)S(1)}, s32[]{:S(2)}) async-start(s8[14155776]{0:T(1024)(128)(4,1)} %bitcast.35), calls=%async_computation | async-start | bytes 3145728
  33.2 15.5 %slice-start.1 = ((s8[14155776]{0:T(1024)(128)(4,1)}), s8[4194304]{0:T(1024)(128)(4,1)S(1)}, s32[]{:S(2)}) async-start(s8[14155776]{0:T(1024)(128)(4,1)} %bitcast.35), calls=%async_computation.1 | async-start | bytes 8388608
  33.2 15.5 %slice-start.2 = ((s8[14155776]{0:T(1024)(128)(4,1)}), s8[4194304]{0:T(1024)(128)(4,1)S(1)}, s32[]{:S(2)}) async-start(s8[14155776]{0:T(1024)(128)(4,1)} %bitcast.35), calls=%async_computation.2 | async-start | bytes 8388608
  33.2 15.5 %slice-start.3 = ((s8[14155776]{0:T(1024)(128)(4,1)}), s8[4194304]{0:T(1024)(128)(4,1)S(1)}, s32[]{:S(2)}) async-start(s8[14155776]{0:T(1024)(128)(4,1)} %bitcast.35), calls=%async_computation.3 | async-start | bytes 8388608
  33.2 12.9 %collective-permute-start.10 = (bf16[96,2048]{1,0:T(8,128)(2,1)S(1)}, bf16[96,2048]{1,0:T(8,128)(2,1)S(1)}, u32[]{:S(2)}, u32[]{:S(2)}) collective-permute-start(bf16[96,2048]{1,0:T(8,128)(2,1)S(1)} %pad_maximum_fusion.2.refs_0_), channel_id=1, source_target_pairs={{0,6},{1,7},{2,0},{3,1},{4,2},{5,3},{6,4},{7,5},{8,14},{9,15},{10,... | collective-permute-start | bytes 1179656 | tf_op jit(solution)/shard_map/ppermute | solution.py:382
  35.2 13.5 %collective-permute-start.11 = (bf16[96,2048]{1,0:T(8,128)(2,1)}, bf16[96,2048]{1,0:T(8,128)(2,1)S(1)}, u32[]{:S(2)}, u32[]{:S(2)}) collective-permute-start(bf16[96,2048]{1,0:T(8,128)(2,1)} %collective-permute-done.9.refs_1_), channel_id=1, source_target_pairs={{0,2},{1,3},{2,4},{3,5},{4,6},{5,7},{6,0},{7,1},{8,10},{9,11},{10,... | collective-permute-start | bytes 1179656 | tf_op jit(solution)/shard_map/ppermute | solution.py:382
  35.3 17.7 %collective-permute-start.8 = (bf16[96,2048]{1,0:T(8,128)(2,1)S(1)}, bf16[96,2048]{1,0:T(8,128)(2,1)S(1)}, u32[]{:S(2)}, u32[]{:S(2)}) collective-permute-start(bf16[96,2048]{1,0:T(8,128)(2,1)S(1)} %collective-permute-done.7.refs_2_), channel_id=1, source_target_pairs={{0,6},{1,7},{2,0},{3,1},{4,2},{5,3},{6,4},{7,5},{8,14},{9,15},{10,... | collective-permute-start | bytes 1179656 | tf_op jit(solution)/shard_map/ppermute | solution.py:382
  38.4 14.5 %collective-permute-start.14 = (bf16[384,384]{1,0:T(8,128)(2,1)}, bf16[384,384]{1,0:T(8,128)(2,1)S(1)}, u32[]{:S(2)}, u32[]{:S(2)}) collective-permute-start(bf16[384,384]{1,0:T(8,128)(2,1)} %refs_1_.1), channel_id=1, source_target_pairs={{0,64},{8,72},{16,80},{24,88},{32,96},{40,104},{48,112},{56,120},{... | collective-permute-start | bytes 884744 | tf_op jit(solution)/shard_map/ppermute | solution.py:373
  39.6 14.4 %collective-permute-start.6 = (bf16[96,2048]{1,0:T(8,128)(2,1)S(1)}, bf16[96,2048]{1,0:T(8,128)(2,1)S(1)}, u32[]{:S(2)}, u32[]{:S(2)}) collective-permute-start(bf16[96,2048]{1,0:T(8,128)(2,1)S(1)} %constant_dynamic-update-slice_fusion.refs_0_), channel_id=1, source_target_pairs={{0,2},{1,3},{2,4},{3,5},{4,6},{5,7},{6,0},{7,1},{8,10},{9,11},{10,... | collective-permute-start | bytes 1179656 | tf_op jit(solution)/shard_map/ppermute | solution.py:382
  52.9 19.7 %copy-start.2 = (f32[4,3,12,384]{3,0,2,1:T(4,128)S(1)}, f32[4,3,12,384]{3,0,2,1:T(4,128)}, u32[]{:S(2)}) copy-start(f32[4,3,12,384]{3,0,2,1:T(4,128)} %reshape.18) | copy-start | bytes 663556
  52.9 21.7 %copy-start.1 = (bf16[384,384]{1,0:T(8,128)(2,1)S(1)}, bf16[384,384]{1,0:T(8,128)(2,1)}, u32[]{:S(2)}) copy-start(bf16[384,384]{1,0:T(8,128)(2,1)} %copy-done) | copy-start | bytes 884740
  57.9 14.8 %collective-permute-start.15 = (bf16[384,768]{1,0:T(8,128)(2,1)S(1)}, bf16[384,768]{1,0:T(8,128)(2,1)S(1)}, u32[]{:S(2)}, u32[]{:S(2)}) collective-permute-start(bf16[384,768]{1,0:T(8,128)(2,1)S(1)} %get-tuple-element.73.kv0.refs_6_.refs_2_), channel_id=1, source_target_pairs={{0,16},{8,24},{16,0},{24,8},{32,48},{40,56},{48,32},{56,40},{64,80... | collective-permute-start | bytes 1769480 | tf_op jit(solution)/shard_map/ppermute | solution.py:376
  58.9 10.5 %collective-permute-start.18 = (bf16[384,384]{1,0:T(8,128)(2,1)S(1)}, bf16[384,384]{1,0:T(8,128)(2,1)S(1)}, u32[]{:S(2)}, u32[]{:S(2)}) collective-permute-start(bf16[384,384]{1,0:T(8,128)(2,1)S(1)} %get-tuple-element.72.q0.refs_0_), channel_id=1, source_target_pairs={{0,64},{8,72},{16,80},{24,88},{32,96},{40,104},{48,112},{56,120},{... | collective-permute-start | bytes 884744 | tf_op jit(solution)/shard_map/ppermute | solution.py:373
  59.5 12.5 %collective-permute-start.17 = (bf16[384,384]{1,0:T(8,128)(2,1)S(1)}, bf16[384,384]{1,0:T(8,128)(2,1)S(1)}, u32[]{:S(2)}, u32[]{:S(2)}) collective-permute-start(bf16[384,384]{1,0:T(8,128)(2,1)S(1)} %get-tuple-element.72.q0.refs_0_), channel_id=1, source_target_pairs={{0,96},{8,104},{16,112},{24,120},{32,0},{40,8},{48,16},{56,24},{64... | collective-permute-start | bytes 884744 | tf_op jit(solution)/shard_map/ppermute | solution.py:373
  61.5 11.2 %collective-permute-start.16 = (bf16[384,384]{1,0:T(8,128)(2,1)S(1)}, bf16[384,384]{1,0:T(8,128)(2,1)S(1)}, u32[]{:S(2)}, u32[]{:S(2)}) collective-permute-start(bf16[384,384]{1,0:T(8,128)(2,1)S(1)} %get-tuple-element.72.q0.refs_0_), channel_id=1, source_target_pairs={{0,32},{8,40},{16,48},{24,56},{32,64},{40,72},{48,80},{56,88},{64,... | collective-permute-start | bytes 884744 | tf_op jit(solution)/shard_map/ppermute | solution.py:373
  61.5 11.2 %collective-permute-start.20 = (bf16[384,768]{1,0:T(8,128)(2,1)S(1)}, bf16[384,768]{1,0:T(8,128)(2,1)S(1)}, u32[]{:S(2)}, u32[]{:S(2)}) collective-permute-start(bf16[384,768]{1,0:T(8,128)(2,1)S(1)} %get-tuple-element.73.kv0.refs_6_.refs_2_), channel_id=1, source_target_pairs={{0,8},{8,0},{16,24},{24,16},{32,40},{40,32},{48,56},{56,48},{64,72... | collective-permute-start | bytes 1769480 | tf_op jit(solution)/shard_map/ppermute | solution.py:379
  72.6 2.0 collective-permute-start.19
  89.5 7.1 %collective-permute-start.23 = (f32[4,9,384]{2,1,0:T(8,128)S(1)}, f32[4,9,384]{2,1,0:T(8,128)S(1)}, u32[]{:S(2)}, u32[]{:S(2)}) collective-permute-start(f32[4,9,384]{2,1,0:T(8,128)S(1)} %get-tuple-element.82.s0), channel_id=1, source_target_pairs={{0,64},{8,72},{16,80},{24,88},{32,96},{40,104},{48,112},{56,120},{... | collective-permute-start | bytes 165896 | tf_op jit(solution)/shard_map/ppermute | solution.py:373
  91.6 5.7 %collective-permute-start.22 = (f32[4,9,384]{2,1,0:T(8,128)S(1)}, f32[4,9,384]{2,1,0:T(8,128)S(1)}, u32[]{:S(2)}, u32[]{:S(2)}) collective-permute-start(f32[4,9,384]{2,1,0:T(8,128)S(1)} %get-tuple-element.82.s0), channel_id=1, source_target_pairs={{0,96},{8,104},{16,112},{24,120},{32,0},{40,8},{48,16},{56,24},{64... | collective-permute-start | bytes 165896 | tf_op jit(solution)/shard_map/ppermute | solution.py:373
  93.3 5.8 %collective-permute-start.21 = (f32[4,9,384]{2,1,0:T(8,128)S(1)}, f32[4,9,384]{2,1,0:T(8,128)S(1)}, u32[]{:S(2)}, u32[]{:S(2)}) collective-permute-start(f32[4,9,384]{2,1,0:T(8,128)S(1)} %get-tuple-element.82.s0), channel_id=1, source_target_pairs={{0,32},{8,40},{16,48},{24,56},{32,64},{40,72},{48,80},{56,88},{64,... | collective-permute-start | bytes 165896 | tf_op jit(solution)/shard_map/ppermute | solution.py:373
  99.3 15.8 %collective-permute-start.26 = (bf16[3,128,384]{2,1,0:T(8,128)(2,1)S(1)}, bf16[3,128,384]{2,1,0:T(8,128)(2,1)S(1)}, u32[]{:S(2)}, u32[]{:S(2)}) collective-permute-start(bf16[3,128,384]{2,1,0:T(8,128)(2,1)S(1)} %get-tuple-element.128), channel_id=1, source_target_pairs={{0,64},{8,72},{16,80},{24,88},{32,96},{40,104},{48,112},{56,120},{... | collective-permute-start | bytes 884744 | tf_op jit(solution)/shard_map/ppermute | solution.py:373
  100.3 14.9 %collective-permute-start.25 = (bf16[3,128,384]{2,1,0:T(8,128)(2,1)S(1)}, bf16[3,128,384]{2,1,0:T(8,128)(2,1)S(1)}, u32[]{:S(2)}, u32[]{:S(2)}) collective-permute-start(bf16[3,128,384]{2,1,0:T(8,128)(2,1)S(1)} %get-tuple-element.129), channel_id=1, source_target_pairs={{0,96},{8,104},{16,112},{24,120},{32,0},{40,8},{48,16},{56,24},{64... | collective-permute-start | bytes 884744 | tf_op jit(solution)/shard_map/ppermute | solution.py:373
  102.0 13.1 %collective-permute-start.24 = (bf16[3,128,384]{2,1,0:T(8,128)(2,1)S(1)}, bf16[3,128,384]{2,1,0:T(8,128)(2,1)S(1)}, u32[]{:S(2)}, u32[]{:S(2)}) collective-permute-start(bf16[3,128,384]{2,1,0:T(8,128)(2,1)S(1)} %get-tuple-element.130), channel_id=1, source_target_pairs={{0,32},{8,40},{16,48},{24,56},{32,64},{40,72},{48,80},{56,88},{64,... | collective-permute-start | bytes 884744 | tf_op jit(solution)/shard_map/ppermute | solution.py:373
  115.2 2.1 %collective-permute-start.27 = (bf16[384,768]{1,0:T(8,128)(2,1)S(1)}, bf16[384,768]{1,0:T(8,128)(2,1)S(1)}, u32[]{:S(2)}, u32[]{:S(2)}) collective-permute-start(bf16[384,768]{1,0:T(8,128)(2,1)S(1)} %get-tuple-element.92), channel_id=1, source_target_pairs={{0,8},{8,0},{16,24},{24,16},{32,40},{40,32},{48,56},{56,48},{64,72... | collective-permute-start | bytes 1769480 | tf_op jit(solution)/shard_map/ppermute | solution.py:379
  117.4 16.4 %collective-permute-start.28 = (bf16[384,768]{1,0:T(8,128)(2,1)S(1)}, bf16[384,768]{1,0:T(8,128)(2,1)S(1)}, u32[]{:S(2)}, u32[]{:S(2)}) collective-permute-start(bf16[384,768]{1,0:T(8,128)(2,1)S(1)} %add.255), channel_id=1, source_target_pairs={{0,16},{8,24},{16,0},{24,8},{32,48},{40,56},{48,32},{56,40},{64,80... | collective-permute-start | bytes 1769480 | tf_op jit(solution)/shard_map/ppermute | solution.py:376
  129.1 11.5 %collective-permute-start.31 = (bf16[384,384]{1,0:T(8,128)(2,1)S(1)}, bf16[384,384]{1,0:T(8,128)(2,1)S(1)}, u32[]{:S(2)}, u32[]{:S(2)}) collective-permute-start(bf16[384,384]{1,0:T(8,128)(2,1)S(1)} %get-tuple-element.132), channel_id=1, source_target_pairs={{0,64},{8,72},{16,80},{24,88},{32,96},{40,104},{48,112},{56,120},{... | collective-permute-start | bytes 884744 | tf_op jit(solution)/shard_map/ppermute | solution.py:373
  131.8 14.3 %collective-permute-start.30 = (bf16[384,384]{1,0:T(8,128)(2,1)S(1)}, bf16[384,384]{1,0:T(8,128)(2,1)S(1)}, u32[]{:S(2)}, u32[]{:S(2)}) collective-permute-start(bf16[384,384]{1,0:T(8,128)(2,1)S(1)} %get-tuple-element.133), channel_id=1, source_target_pairs={{0,96},{8,104},{16,112},{24,120},{32,0},{40,8},{48,16},{56,24},{64... | collective-permute-start | bytes 884744 | tf_op jit(solution)/shard_map/ppermute | solution.py:373
  133.4 12.7 %collective-permute-start.29 = (bf16[384,384]{1,0:T(8,128)(2,1)S(1)}, bf16[384,384]{1,0:T(8,128)(2,1)S(1)}, u32[]{:S(2)}, u32[]{:S(2)}) collective-permute-start(bf16[384,384]{1,0:T(8,128)(2,1)S(1)} %get-tuple-element.134), channel_id=1, source_target_pairs={{0,32},{8,40},{16,48},{24,56},{32,64},{40,72},{48,80},{56,88},{64,... | collective-permute-start | bytes 884744 | tf_op jit(solution)/shard_map/ppermute | solution.py:373
  146.1 2.0 collective-permute-start.32
  156.5 22.7 %collective-permute-start.33 = (bf16[192,2048]{1,0:T(8,128)(2,1)S(1)}, bf16[192,2048]{1,0:T(8,128)(2,1)S(1)}, u32[]{:S(2)}, u32[]{:S(2)}) collective-permute-start(bf16[192,2048]{1,0:T(8,128)(2,1)S(1)} %get-tuple-element.115), channel_id=1, source_target_pairs={{0,1},{1,0},{2,3},{3,2},{4,5},{5,4},{6,7},{7,6},{8,9},{9,8},{10,11... | collective-permute-start | bytes 2359304 | tf_op jit(solution)/shard_map/ppermute | solution.py:385
  158.4 13.1 %collective-permute-start.39 = (bf16[96,2048]{1,0:T(8,128)(2,1)S(1)}, bf16[96,2048]{1,0:T(8,128)(2,1)S(1)}, u32[]{:S(2)}, u32[]{:S(2)}) collective-permute-start(bf16[96,2048]{1,0:T(8,128)(2,1)S(1)} %get-tuple-element.124), channel_id=1, source_target_pairs={{0,2},{1,3},{2,4},{3,5},{4,6},{5,7},{6,0},{7,1},{8,10},{9,11},{10,... | collective-permute-start | bytes 1179656 | tf_op jit(solution)/shard_map/ppermute | solution.py:382
  165.2 12.1 %collective-permute-start.34 = (bf16[96,2048]{1,0:T(8,128)(2,1)S(1)}, bf16[96,2048]{1,0:T(8,128)(2,1)S(1)}, u32[]{:S(2)}, u32[]{:S(2)}) collective-permute-start(bf16[96,2048]{1,0:T(8,128)(2,1)S(1)} %get-tuple-element.117), channel_id=1, source_target_pairs={{0,6},{1,7},{2,0},{3,1},{4,2},{5,3},{6,4},{7,5},{8,14},{9,15},{10,... | collective-permute-start | bytes 1179656 | tf_op jit(solution)/shard_map/ppermute | solution.py:382
  165.8 20.0 %collective-permute-start.38 = (bf16[96,2048]{1,0:T(8,128)(2,1)S(1)}, bf16[96,2048]{1,0:T(8,128)(2,1)S(1)}, u32[]{:S(2)}, u32[]{:S(2)}) collective-permute-start(bf16[96,2048]{1,0:T(8,128)(2,1)S(1)} %get-tuple-element.122), channel_id=1, source_target_pairs={{0,6},{1,7},{2,0},{3,1},{4,2},{5,3},{6,4},{7,5},{8,14},{9,15},{10,... | collective-permute-start | bytes 1179656 | tf_op jit(solution)/shard_map/ppermute | solution.py:382
  166.6 22.8 %collective-permute-start.42 = (bf16[96,2048]{1,0:T(8,128)(2,1)S(1)}, bf16[96,2048]{1,0:T(8,128)(2,1)S(1)}, u32[]{:S(2)}, u32[]{:S(2)}) collective-permute-start(bf16[96,2048]{1,0:T(8,128)(2,1)S(1)} %get-tuple-element.126), channel_id=1, source_target_pairs={{0,2},{1,3},{2,4},{3,5},{4,6},{5,7},{6,0},{7,1},{8,10},{9,11},{10,... | collective-permute-start | bytes 1179656 | tf_op jit(solution)/shard_map/ppermute | solution.py:382
  171.5 16.7 %collective-permute-start.40 = (bf16[96,2048]{1,0:T(8,128)(2,1)S(1)}, bf16[96,2048]{1,0:T(8,128)(2,1)S(1)}, u32[]{:S(2)}, u32[]{:S(2)}) collective-permute-start(bf16[96,2048]{1,0:T(8,128)(2,1)S(1)} %add.269), channel_id=1, source_target_pairs={{0,2},{1,3},{2,4},{3,5},{4,6},{5,7},{6,0},{7,1},{8,10},{9,11},{10,... | collective-permute-start | bytes 1179656 | tf_op jit(solution)/shard_map/ppermute | solution.py:382
  177.4 17.5 %collective-permute-start.43 = (bf16[96,2048]{1,0:T(8,128)(2,1)S(1)}, bf16[96,2048]{1,0:T(8,128)(2,1)S(1)}, u32[]{:S(2)}, u32[]{:S(2)}) collective-permute-start(bf16[96,2048]{1,0:T(8,128)(2,1)S(1)} %add.273), channel_id=1, source_target_pairs={{0,6},{1,7},{2,0},{3,1},{4,2},{5,3},{6,4},{7,5},{8,14},{9,15},{10,... | collective-permute-start | bytes 1179656 | tf_op jit(solution)/shard_map/ppermute | solution.py:382
  179.3 18.9 %collective-permute-start.35 = (bf16[48,2048]{1,0:T(8,128)(2,1)S(1)}, bf16[48,2048]{1,0:T(8,128)(2,1)S(1)}, u32[]{:S(2)}, u32[]{:S(2)}) collective-permute-start(bf16[48,2048]{1,0:T(8,128)(2,1)S(1)} %get-tuple-element.135), channel_id=1, source_target_pairs={{0,2},{1,3},{2,4},{3,5},{4,6},{5,7},{6,0},{7,1},{8,10},{9,11},{10,... | collective-permute-start | bytes 589832 | tf_op jit(solution)/shard_map/ppermute | solution.py:382
  185.7 12.5 %collective-permute-start.37 = (bf16[48,2048]{1,0:T(8,128)(2,1)S(1)}, bf16[48,2048]{1,0:T(8,128)(2,1)S(1)}, u32[]{:S(2)}, u32[]{:S(2)}) collective-permute-start(bf16[48,2048]{1,0:T(8,128)(2,1)S(1)} %get-tuple-element.136), channel_id=1, source_target_pairs={{0,4},{1,5},{2,6},{3,7},{4,0},{5,1},{6,2},{7,3},{8,12},{9,13},{10,... | collective-permute-start | bytes 589832 | tf_op jit(solution)/shard_map/ppermute | solution.py:382
  188.3 12.9 %collective-permute-start.36 = (bf16[48,2048]{1,0:T(8,128)(2,1)S(1)}, bf16[48,2048]{1,0:T(8,128)(2,1)S(1)}, u32[]{:S(2)}, u32[]{:S(2)}) collective-permute-start(bf16[48,2048]{1,0:T(8,128)(2,1)S(1)} %get-tuple-element.137), channel_id=1, source_target_pairs={{0,6},{1,7},{2,0},{3,1},{4,2},{5,3},{6,4},{7,5},{8,14},{9,15},{10,... | collective-permute-start | bytes 589832 | tf_op jit(solution)/shard_map/ppermute | solution.py:382
  189.4 11.9 %collective-permute-start.41 = (bf16[48,2048]{1,0:T(8,128)(2,1)S(1)}, bf16[48,2048]{1,0:T(8,128)(2,1)S(1)}, u32[]{:S(2)}, u32[]{:S(2)}) collective-permute-start(bf16[48,2048]{1,0:T(8,128)(2,1)S(1)} %slice.108), channel_id=1, source_target_pairs={{0,1},{1,0},{2,3},{3,2},{4,5},{5,4},{6,7},{7,6},{8,9},{9,8},{10,11... | collective-permute-start | bytes 589832 | tf_op jit(solution)/shard_map/ppermute | solution.py:385
  195.1 7.3 %collective-permute-start.44 = (bf16[48,2048]{1,0:T(8,128)(2,1)S(1)}, bf16[48,2048]{1,0:T(8,128)(2,1)S(1)}, u32[]{:S(2)}, u32[]{:S(2)}) collective-permute-start(bf16[48,2048]{1,0:T(8,128)(2,1)S(1)} %slice.107), channel_id=1, source_target_pairs={{0,1},{1,0},{2,3},{3,2},{4,5},{5,4},{6,7},{7,6},{8,9},{9,8},{10,11... | collective-permute-start | bytes 589832 | tf_op jit(solution)/shard_map/ppermute | solution.py:385
